TPU v7x, 256 devices: a whole 4x4x8 slice. The times are simulated.
256 devices in a mesh: gx: 16 (over z_hi, y), gy: 16 (over x, z_lo, core).
Axes of the slice: x: 4, y: 4, z: 8 (z_hi: 4, z_lo: 2; z = z_hi * 2 + z_lo), core: 2. Of those that a mesh axis runs over, the one named last changes fastest.
Arguments:
- prec_pops: float32 [27, 64, 128, 256], P(None, 'gx', 'gy'), may hold values from 0 to 1, as said below
- main_pops: float32 [27, 128, 256, 256], P(None, 'gx', 'gy'), may hold values from 0 to 1, as said below
- cell_type: int32 [128, 256, 256], P('gx', 'gy'), may hold values from 0 to 2, as said below
- rates: float32 [27], replicated, may hold values from 0.7 to 1.8
Outputs:
- prec_next: float32 [27, 64, 128, 256], P(None, 'gx', 'gy')
- main_next: float32 [27, 128, 256, 256], P(None, 'gx', 'gy')
Inputs may be any that keep to these rules, and one draw needn't show every extreme that they name: `prec_pops`: every population is positive; the populations of a cell sum to between 0.6 and 1.5. `main_pops`: every population is positive; the populations of a cell sum to between 0.6 and 1.5. `cell_type`: the lowest one to three cells of every column are solid (1); above them cells are fluid (0) or turbine disk (2).
All inputs are finite; a program needn't handle non-finite values.
Results may differ from a plain program's by a relative error of at most 0.000076.
Values sent between devices are 32-bit elements; how exact they have to be, the bound alone decides.
A program may use at most 128 MiB of HBM per device.

v0:
```python
import functools

import jax
import jax.numpy as jnp
from jax import lax
from jax.experimental import pallas as pl
from jax.experimental.pallas import tpu as pltpu
from jax.sharding import PartitionSpec as P

MESH = pl.DeviceIdType.MESH
F32 = jnp.float32
LANES = 128
ROWS = 8
TOP = 8


def scale_of(moment):
    a, b, e = moment // 9, moment // 3 % 3, moment % 3
    return (0.5 if a else 1.0) * (0.5 if b else 1.0) * (0.5 if e else 1.0)


def third_of(moment):
    a, b, e = moment // 9, moment // 3 % 3, moment % 3
    return (1.0 / 3.0) ** ((a == 2) + (b == 2) + (e == 2))


def axis_triples():
    for stride in (9, 3, 1):
        for base in range(27):
            if base // stride % 3 == 0:
                yield base, base + stride, base + 2 * stride


def to_moments(f):
    m = list(f)
    for low, mid, high in axis_triples():
        total = m[high] + m[low]
        m[low], m[mid], m[high] = total + m[mid], m[high] - m[low], total
    return m


def to_populations(m):
    g = list(m)
    for low, mid, high in axis_triples():
        g[low], g[mid], g[high] = g[high] - g[mid], g[low] - (g[high] + g[high]), g[high] + g[mid]
    return g


def collide(f, keep, gain, disk=None):
    m = to_moments(f)
    rho, jx, jy, jz = m[0], m[9], m[3], m[1]
    inverse = 1.0 / rho
    ux, uy, uz = jx * inverse, jy * inverse, jz * inverse
    qx, qy, qz = jx * ux, jy * uy, jz * uz
    third = rho * (1.0 / 3.0)
    ex, ey, ez = third + qx, third + qy, third + qz
    exy, exz, eyz = ex + qy, ex + qz, ey + qz
    even = {18: ex, 6: ey, 2: ez, 24: exy, 20: exz, 8: eyz, 26: exy + qz}
    odd = {}
    for k in range(27):
        a, b, e = k // 9, k // 3 % 3, k % 3
        ones = (a == 1) + (b == 1) + (e == 1)
        if ones == 1:
            odd[k] = jx if a == 1 else jy if b == 1 else jz
        elif ones == 2:
            odd[k] = jx * uy if e != 1 else jx * uz if b != 1 else jy * uz
    out = [None] * 27
    shared = {}
    for k in range(27):
        a, b, e = k // 9, k // 3 % 3, k % 3
        if k == 0:
            out[k] = rho
        elif k in (9, 3, 1):
            out[k] = odd[k] * 0.5
        elif k == 13:
            out[k] = keep(k) * m[k]
        elif k in even:
            out[k] = keep(k) * m[k] + gain(k) * even[k]
        else:
            pair = (a == 1, b == 1, e == 1)
            if pair not in shared:
                shared[pair] = odd[k]
            out[k] = keep(k) * m[k] + gain(k) * shared[pair]
    if disk is not None:
        drag = jnp.where(disk, (-0.5 * 0.75) * jx * jnp.abs(ux), 0.0)
        out[9] = out[9] + drag * 0.5
        side = drag * (0.25 / 3.0)
        out[15] = out[15] + side
        out[11] = out[11] + side
        out[17] = out[17] + drag * (0.125 / 9.0)
    return to_populations(out)


def even_orders(k):
    a, b, e = k // 9, k // 3 % 3, k % 3
    return a != 1 and b != 1 and e != 1


def rows_across(g, i, part, row):
    planes, ztiles, pitch = g.shape[2:5]
    flat = g.reshape(27 * planes * ztiles * pitch, LANES)
    return flat, pl.ds(((i * planes + 1) * ztiles + part * ROWS) * pitch + row, ROWS, stride=pitch)


def load_across(g, i, part, row):
    flat, rows = rows_across(g, i, part, row)
    return flat[rows, :]


def store_across(g, i, part, row, value):
    flat, rows = rows_across(g, i, part, row)
    flat[rows, :] = value


def exchange(
    size,
    rates,
    prec_hbm,
    main_hbm,
    cell_hbm,
    main_g,
    prec_g,
    main_in,
    prec_in,
    cell_in,
    table,
    main_out_y,
    main_got_y,
    main_out_c,
    main_got_c,
    prec_out_y,
    prec_got_y,
    prec_out_c,
    prec_got_c,
    load_sem,
    cell_sem,
    main_send,
    main_recv,
    prec_send,
    prec_recv,
    extra_send,
):
    nx, ny = size
    gx, gy = lax.axis_index("gx"), lax.axis_index("gy")
    main_x, main_y = main_in.shape[1], main_in.shape[2]
    prec_x, prec_y = prec_in.shape[1], prec_in.shape[2]
    ztiles = main_g.shape[3]
    first, last = gx == 0, gx == nx - 1
    east, west = lax.rem(gx + 1, nx), lax.rem(gx + nx - 1, nx)
    north, south = lax.rem(gy + 1, ny), lax.rem(gy + ny - 1, ny)
    half = ny // 2

    barrier = pltpu.get_barrier_semaphore()
    for other in (
        (west, gy), (east, gy), (gx, south), (gx, north),
        (west, south), (west, north), (east, south), (east, north),
    ):
        pl.semaphore_signal(barrier, inc=1, device_id=other, device_id_type=MESH)

    @pl.when(first)
    def _():
        for block in (2 * gy, 2 * gy + 1, 2 * gy + ny - 1, 2 * gy + 2):
            pl.semaphore_signal(
                barrier, inc=1, device_id=(nx - 1, lax.rem(block, ny)), device_id_type=MESH
            )

    def main_load(x):
        return pltpu.make_async_copy(main_hbm.at[:, x], main_in.at[:, x], load_sem.at[x])

    def prec_load(x):
        return pltpu.make_async_copy(prec_hbm.at[:, x], prec_in.at[:, x], load_sem.at[main_x + x])

    cell_load = pltpu.make_async_copy(cell_hbm, cell_in, cell_sem)
    cell_load.start()
    main_load(main_x - 1).start()
    main_load(0).start()
    prec_load(prec_x - 1).start()
    prec_load(0).start()
    for x in range(1, main_x - 1):
        main_load(x).start()
    for x in range(1, prec_x - 1):
        prec_load(x).start()

    for k in range(27):
        rate = rates[k]
        kept = scale_of(k) * (1.0 - rate)
        table[k] = jnp.full((ROWS, LANES), kept, F32)
        factor = third_of(k) * (3.0 if even_orders(k) else 1.0)
        table[27 + k] = jnp.full((ROWS, LANES), scale_of(k) * factor * rate, F32)

    def keep(k):
        return table[k]

    def gain(k):
        return table[27 + k]

    def tile_of(step):
        row = pl.multiple_of(lax.div(step, ztiles) * ROWS, ROWS)
        z = lax.rem(step, ztiles)
        return row, z, pl.multiple_of(z * LANES, LANES)

    def main_plane(x):
        def body(step, carry):
            row, z, lane = tile_of(step)
            rows, lanes = pl.ds(row, ROWS), pl.ds(lane, LANES)
            flags = cell_in[x, rows, lanes]
            g = collide([main_in[i, x, rows, lanes] for i in range(27)], keep, gain, flags == 2)
            solid = flags == 1
            for i in range(27):
                value = jnp.where(solid, main_in[26 - i, x, rows, lanes], g[i])
                main_g[i // 9, i % 9, x + 1, z, pl.ds(pl.multiple_of(TOP + row, ROWS), ROWS), :] = value
            return carry

        lax.fori_loop(0, main_y // ROWS * ztiles, body, 0)

    def prec_plane(x):
        def body(step, carry):
            row, z, lane = tile_of(step)
            rows, lanes = pl.ds(row, ROWS), pl.ds(lane, LANES)
            g = collide([prec_in[i, x, rows, lanes] for i in range(27)], keep, gain)
            for i in range(27):
                prec_g[i // 9, i % 9, x + 1, z, pl.ds(pl.multiple_of(TOP + row, ROWS), ROWS), :] = g[i]
            return carry

        lax.fori_loop(0, prec_y // ROWS * ztiles, body, 0)

    def remote(src, dst, send, recv, device):
        return pltpu.make_async_remote_copy(
            src_ref=src, dst_ref=dst, send_sem=send, recv_sem=recv, device_id=device, device_id_type=MESH
        )

    def x_face(g, count, rows, east_side, send, recv):
        inner = pl.ds(TOP, rows)
        if east_side:
            return remote(g.at[2, :, count, :, inner], g.at[2, :, 0, :, inner], send.at[0], recv.at[0], (east, gy))
        return remote(g.at[0, :, 1, :, inner], g.at[0, :, count + 1, :, inner], send.at[1], recv.at[1], (west, gy))

    main_east = x_face(main_g, main_x, main_y, True, main_send, main_recv)
    main_west = x_face(main_g, main_x, main_y, False, main_send, main_recv)
    prec_east = x_face(prec_g, prec_x, prec_y, True, prec_send, prec_recv)
    prec_west = x_face(prec_g, prec_x, prec_y, False, prec_send, prec_recv)

    def inlet(target):
        place = pl.ds(pl.multiple_of(TOP + lax.rem(gy, 2) * prec_y, ROWS), prec_y)
        return remote(
            prec_g.at[2, :, prec_x, :, pl.ds(TOP, prec_y)],
            main_g.at[2, :, 0, :, place],
            extra_send.at[target],
            main_recv.at[0],
            (0, lax.div(gy, 2) + target * half),
        )

    main_load(main_x - 1).wait()
    cell_load.wait()
    main_plane(main_x - 1)
    pl.semaphore_wait(barrier, jnp.where(last, 12, 8))

    @pl.when(jnp.logical_not(last))
    def _():
        main_east.start()

    main_load(0).wait()
    main_plane(0)

    @pl.when(jnp.logical_not(first))
    def _():
        main_west.start()

    prec_load(prec_x - 1).wait()
    prec_plane(prec_x - 1)
    prec_east.start()

    @pl.when(last)
    def _():
        inlet(0).start()
        inlet(1).start()

    prec_load(0).wait()
    prec_plane(0)
    prec_west.start()

    def prec_rest(x, carry):
        prec_load(x).wait()
        prec_plane(x)
        return carry

    lax.fori_loop(1, prec_x - 1, prec_rest, 0)

    def pack(g, count, rows, out_y, out_c):
        for side in range(2):
            row = TOP + rows - 1 if side == 0 else TOP
            for a in range(3):
                for e in range(3):
                    i = 9 * a + (6 if side == 0 else 0) + e
                    for part in range(count * ztiles // ROWS):
                        out_y[side, 3 * a + e, pl.ds(part * ROWS, ROWS), :] = load_across(g, i, part, row)
        for corner in range(4):
            side, a, x = corner % 2, 2 if corner < 2 else 0, count if corner < 2 else 1
            row = TOP + rows - 1 if side == 0 else TOP
            for e in range(3):
                for z in range(ztiles):
                    out_c[corner, pl.ds(e * ztiles + z, 1), :] = g[a, (6 if side == 0 else 0) + e, x, z, pl.ds(row, 1), :]

    def y_copies(out_y, got_y, send, recv):
        return [
            remote(out_y.at[side], got_y.at[side], send.at[2 + side], recv.at[2 + side], (gx, (north, south)[side]))
            for side in range(2)
        ]

    def corner_copies(out_c, got_c, send, recv):
        return [
            remote(
                out_c.at[corner], got_c.at[corner], send.at[4 + corner], recv.at[4 + corner],
                (east if corner < 2 else west, (north, south)[corner % 2]),
            )
            for corner in range(4)
        ]

    def inlet_corner(corner, target):
        block = lax.rem(lax.div(gy + 1, 2), half) if corner == 0 else lax.rem(lax.div(gy, 2) + half - 1, half)
        return remote(
            prec_out_c.at[corner], main_got_c.at[corner], extra_send.at[2 + target], main_recv.at[4 + corner],
            (0, block + target * half),
        )

    pack(prec_g, prec_x, prec_y, prec_out_y, prec_out_c)
    prec_y_copies = y_copies(prec_out_y, prec_got_y, prec_send, prec_recv)
    prec_corners = corner_copies(prec_out_c, prec_got_c, prec_send, prec_recv)
    main_y_copies = y_copies(main_out_y, main_got_y, main_send, main_recv)
    main_corners = corner_copies(main_out_c, main_got_c, main_send, main_recv)
    odd = lax.rem(gy, 2) == 1
    for copy in prec_y_copies + prec_corners:
        copy.start()

    @pl.when(jnp.logical_and(last, odd))
    def _():
        inlet_corner(0, 0).start()
        inlet_corner(0, 1).start()

    @pl.when(jnp.logical_and(last, jnp.logical_not(odd)))
    def _():
        inlet_corner(1, 0).start()
        inlet_corner(1, 1).start()

    def main_rest(x, carry):
        main_load(x).wait()
        main_plane(x)
        return carry

    lax.fori_loop(1, main_x - 1, main_rest, 0)
    pack(main_g, main_x, main_y, main_out_y, main_out_c)
    for copy in main_y_copies:
        copy.start()

    @pl.when(jnp.logical_not(last))
    def _():
        main_corners[0].start()
        main_corners[1].start()

    @pl.when(jnp.logical_not(first))
    def _():
        main_corners[2].start()
        main_corners[3].start()

    def unpack(g, count, rows, got_y):
        for side in range(2):
            row = TOP - 1 if side == 0 else TOP + rows
            for a in range(3):
                for e in range(3):
                    i = 9 * a + (6 if side == 0 else 0) + e
                    for part in range(count * ztiles // ROWS):
                        store_across(g, i, part, row, got_y[side, 3 * a + e, pl.ds(part * ROWS, ROWS), :])

    def unpack_corner(g, count, rows, got_c, corner):
        side, a, x = corner % 2, 2 if corner < 2 else 0, 0 if corner < 2 else count + 1
        row = TOP - 1 if side == 0 else TOP + rows
        for e in range(3):
            for z in range(ztiles):
                g[a, (6 if side == 0 else 0) + e, x, z, pl.ds(row, 1), :] = got_c[corner, pl.ds(e * ztiles + z, 1), :]

    for side in range(2):
        prec_y_copies[side].wait_recv()
    unpack(prec_g, prec_x, prec_y, prec_got_y)
    for corner in range(4):
        prec_corners[corner].wait_recv()
        unpack_corner(prec_g, prec_x, prec_y, prec_got_c, corner)
    for side in range(2):
        main_y_copies[side].wait_recv()
    unpack(main_g, main_x, main_y, main_got_y)
    for corner in range(2):
        main_corners[corner].wait_recv()
        unpack_corner(main_g, main_x, main_y, main_got_c, corner)

    @pl.when(jnp.logical_not(last))
    def _():
        for corner in range(2, 4):
            main_corners[corner].wait_recv()
            unpack_corner(main_g, main_x, main_y, main_got_c, corner)

    prec_east.wait_recv()
    prec_west.wait_recv()
    main_east.wait_recv()

    @pl.when(jnp.logical_not(last))
    def _():
        main_west.wait_recv()

    for copy in [prec_east, prec_west, *prec_y_copies, *prec_corners, *main_y_copies]:
        copy.wait_send()

    @pl.when(jnp.logical_not(last))
    def _():
        for copy in (main_east, main_corners[0], main_corners[1]):
            copy.wait_send()

    @pl.when(jnp.logical_not(first))
    def _():
        for copy in (main_west, main_corners[2], main_corners[3]):
            copy.wait_send()

    @pl.when(last)
    def _():
        for target in range(2):
            inlet(target).wait_send()
            inlet_corner(0, target).wait_send()


def stream(nx, main_g, prec_g, prec_next, main_next, prec_out, main_out, prec_sem, main_sem):
    last = lax.axis_index("gx") == nx - 1

    def plane(g, out, count, rows, x, clamp):
        lane = lax.broadcasted_iota(jnp.int32, (ROWS, LANES), 1)
        low, high = lane == 0, lane == LANES - 1
        ztiles = g.shape[3]

        def body(step, carry):
            row = pl.multiple_of(step * ROWS, ROWS)
            for i in range(27):
                cx, cy, cz = i // 9 - 1, i // 3 % 3 - 1, i % 3 - 1
                source = x + 1 - cx
                if clamp and cx == -1:
                    source = jnp.where(last, jnp.minimum(source, count), source)
                tiles = [g[i // 9, i % 9, source, z, pl.ds(TOP - cy + row, ROWS), :] for z in range(ztiles)]
                if cz:
                    j = 26 - i
                    wall = 0 if cz == 1 else ztiles - 1
                    bounced = g[j // 9, j % 9, x + 1, wall, pl.ds(pl.multiple_of(TOP + row, ROWS), ROWS), :]
                    moved = [pltpu.roll(tile, 1 if cz == 1 else LANES - 1, 1) for tile in tiles]
                    if cz == 1:
                        tiles = [jnp.where(low, moved[z - 1] if z else bounced, moved[z]) for z in range(ztiles)]
                    else:
                        tiles = [
                            jnp.where(high, moved[z + 1] if z < ztiles - 1 else bounced, moved[z])
                            for z in range(ztiles)
                        ]
                for z in range(ztiles):
                    out[x, i, pl.ds(row, ROWS), pl.ds(z * LANES, LANES)] = tiles[z]
            return carry

        lax.fori_loop(0, rows // ROWS, body, 0)

    def run(g, out, dest, sem, clamp):
        count, rows = out.shape[0], out.shape[2]

        def copy(x):
            return pltpu.make_async_copy(out.at[x], dest.at[:, x], sem.at[x])

        def body(x, carry):
            plane(g, out, count, rows, x, clamp)
            copy(x).start()
            return carry

        lax.fori_loop(0, count, body, 0)
        return copy

    main_copy = run(main_g, main_out, main_next, main_sem, True)
    prec_copy = run(prec_g, prec_out, prec_next, prec_sem, False)
    for x in range(main_out.shape[0]):
        main_copy(x).wait()
    for x in range(prec_out.shape[0]):
        prec_copy(x).wait()


def solution(mesh):
    nx, ny = mesh.shape["gx"], mesh.shape["gy"]

    def shards(prec_pops, main_pops, cell_type, rates):
        main_x, main_y, depth = main_pops.shape[1:]
        prec_x, prec_y = prec_pops.shape[1:3]
        ztiles = depth // LANES
        main_shape = (3, 9, main_x + 2, ztiles, main_y + 2 * TOP, LANES)
        prec_shape = (3, 9, prec_x + 2, ztiles, prec_y + 2 * TOP, LANES)
        in_hbm = pl.BlockSpec(memory_space=pltpu.HBM)
        on_chip = pl.BlockSpec(memory_space=pltpu.VMEM)
        main_g, prec_g = pl.pallas_call(
            functools.partial(exchange, (nx, ny)),
            name="exchange",
            out_shape=(pltpu.VMEM(main_shape, F32), pltpu.VMEM(prec_shape, F32)),
            in_specs=[pl.BlockSpec(memory_space=pltpu.SMEM), in_hbm, in_hbm, in_hbm],
            out_specs=(on_chip, on_chip),
            scratch_shapes=[
                pltpu.VMEM(main_pops.shape, F32),
                pltpu.VMEM(prec_pops.shape, F32),
                pltpu.VMEM(cell_type.shape, jnp.int32),
                pltpu.VMEM((54, ROWS, LANES), F32),
                pltpu.VMEM((2, 9, main_x * ztiles, LANES), F32),
                pltpu.VMEM((2, 9, main_x * ztiles, LANES), F32),
                pltpu.VMEM((4, ROWS, LANES), F32),
                pltpu.VMEM((4, ROWS, LANES), F32),
                pltpu.VMEM((2, 9, prec_x * ztiles, LANES), F32),
                pltpu.VMEM((2, 9, prec_x * ztiles, LANES), F32),
                pltpu.VMEM((4, ROWS, LANES), F32),
                pltpu.VMEM((4, ROWS, LANES), F32),
                pltpu.SemaphoreType.DMA((main_x + prec_x,)),
                pltpu.SemaphoreType.DMA,
                pltpu.SemaphoreType.DMA((8,)),
                pltpu.SemaphoreType.DMA((8,)),
                pltpu.SemaphoreType.DMA((8,)),
                pltpu.SemaphoreType.DMA((8,)),
                pltpu.SemaphoreType.DMA((4,)),
            ],
            compiler_params=pltpu.CompilerParams(
                collective_id=0, has_side_effects=True, vmem_limit_bytes=24 * 1024 * 1024
            ),
        )(*(pltpu.with_memory_space_constraint(x, pltpu.HBM) for x in (rates, prec_pops, main_pops, cell_type)))
        prec_next, main_next = pl.pallas_call(
            functools.partial(stream, nx),
            name="stream",
            out_shape=(
                jax.ShapeDtypeStruct(prec_pops.shape, F32),
                jax.ShapeDtypeStruct(main_pops.shape, F32),
            ),
            in_specs=[on_chip, on_chip],
            out_specs=(in_hbm, in_hbm),
            scratch_shapes=[
                pltpu.VMEM((prec_x, 27, prec_y, depth), F32),
                pltpu.VMEM((main_x, 27, main_y, depth), F32),
                pltpu.SemaphoreType.DMA((prec_x,)),
                pltpu.SemaphoreType.DMA((main_x,)),
            ],
            compiler_params=pltpu.CompilerParams(vmem_limit_bytes=24 * 1024 * 1024),
        )(main_g, prec_g)
        return prec_next, main_next

    placed = (P(None, "gx", "gy", None), P(None, "gx", "gy", None), P("gx", "gy", None), P())
    return jax.shard_map(
        shards,
        mesh=mesh,
        in_specs=placed,
        out_specs=(P(None, "gx", "gy", None), P(None, "gx", "gy", None)),
        check_vma=False,
    )
```

profile of v0, /device:TPU:33, one launch (start us, length us, event | category | flops | bytes accessed | tf_op | source)
XLA Modules:
  0.0 30.4 jit_solution(6360149700012670555)
XLA Ops:
  0.6 26.7 %exchange.1 = (f32[3,9,10,2,32,128]{5,4,3,2,1,0:T(8,128)S(1)}, f32[3,9,6,2,24,128]{5,4,3,2,1,0:T(8,128)S(1)}) custom-call(f32[27]{0:T(128)} %rates.1, f32[27,4,8,256]{3,2,1,0:T(8,128)} %prec_hbm.1, f32[27,8,16,256]{3,2,1,0:T(8,128)} %main_hbm.1, s32[8,16,256]{2,1,0:T(8,128)} %cell_hbm.1), custom_call_target="tpu_custom_call" | custom-call | tf_op jit(solution)/shard_map/exchange/pallas_call | solution.py:495
  27.4 3.0 %stream.1 = (f32[27,4,8,256]{3,2,1,0:T(8,128)}, f32[27,8,16,256]{3,2,1,0:T(8,128)}) custom-call(f32[3,9,10,2,32,128]{5,4,3,2,1,0:T(8,128)S(1)} %get-tuple-element.4.main_g, f32[3,9,6,2,24,128]{5,4,3,2,1,0:T(8,128)S(1)} %get-tuple-element.5.prec_g), custom_call_target="tpu_custom_call" | custom-call | tf_op jit(solution)/shard_map/stream/pallas_call | solution.py:526
where the time goes:
time: 30.5 us; the launch traced here: 30.4 us
  Pallas kernels  29.7 us (97%)
  between operations  0.64 us (2%)
    pallas_call x1, Pallas kernels, shards(): pl.pallas_call(functools.partial(exchange, (nx, ny)), name='exchange', ou...  26.7 us
    pallas_call x1, Pallas kernels, shards(): pl.pallas_call(functools.partial(stream, nx), name='stream', out_shape=(j...  3.02 us

commit v1 on v0

--- a/solution.py
+++ b/solution.py
@@ -11,6 +11,7 @@
 F32 = jnp.float32
 LANES = 128
 ROWS = 8
+GROUP = 4
 TOP = 8
 
 
@@ -138,7 +139,11 @@
     main_recv,
     prec_send,
     prec_recv,
-    extra_send,
+    inlet_send,
+    inlet_c,
+    main_relay,
+    prec_relay,
+    relay_recv,
 ):
     nx, ny = size
     gx, gy = lax.axis_index("gx"), lax.axis_index("gy")
@@ -150,19 +155,56 @@
     north, south = lax.rem(gy + 1, ny), lax.rem(gy + ny - 1, ny)
     half = ny // 2
 
+    place = lax.rem(gx, GROUP)
+    up_source = jnp.logical_and(place == GROUP - 1, jnp.logical_not(last))
+    down_source = jnp.logical_and(place == 0, jnp.logical_not(first))
+    up_relay = jnp.logical_and(place == 0, gx + GROUP < nx)
+    down_relay = jnp.logical_and(place == GROUP - 1, gx - GROUP >= 0)
+    crossing = jnp.logical_or(up_source, down_source)
+    relaying = jnp.logical_or(up_relay, down_relay)
+    relay_from = jnp.where(up_relay, gx + GROUP - 1, gx - GROUP + 1)
+    relay_to = jnp.where(up_relay, gx + GROUP, gx - GROUP)
+    relay_of = jnp.where(up_source, gx - GROUP + 1, gx + GROUP - 1)
+    relay_back = jnp.where(down_source, gx - GROUP, gx + GROUP)
+
+    odd = lax.rem(gy, 2) == 1
+    corner_block = jnp.where(odd, lax.rem(lax.div(gy + 1, 2), half), lax.rem(lax.div(gy, 2) + half - 1, half))
+    inlet_targets = [lax.div(gy, 2), lax.div(gy, 2) + half, corner_block, corner_block + half]
+
     barrier = pltpu.get_barrier_semaphore()
+
+    def greet(device):
+        pl.semaphore_signal(barrier, inc=1, device_id=device, device_id_type=MESH)
+
     for other in (
         (west, gy), (east, gy), (gx, south), (gx, north),
         (west, south), (west, north), (east, south), (east, north),
     ):
-        pl.semaphore_signal(barrier, inc=1, device_id=other, device_id_type=MESH)
+        greet(other)
+
+    @pl.when(relaying)
+    def _():
+        greet((relay_from, gy))
+
+    @pl.when(crossing)
+    def _():
+        greet((relay_back, gy))
 
     @pl.when(first)
     def _():
         for block in (2 * gy, 2 * gy + 1, 2 * gy + ny - 1, 2 * gy + 2):
-            pl.semaphore_signal(
-                barrier, inc=1, device_id=(nx - 1, lax.rem(block, ny)), device_id_type=MESH
-            )
+            source = lax.rem(block, ny)
+
+            @pl.when(source != gy)
+            def _():
+                greet((0, source))
+
+    def one_if(condition):
+        return jnp.where(condition, 1, 0)
+
+    greetings = 8 + one_if(relaying) + one_if(crossing)
+    for target in inlet_targets:
+        greetings = greetings + one_if(jnp.logical_and(first, target != gy))
 
     def main_load(x):
         return pltpu.make_async_copy(main_hbm.at[:, x], main_in.at[:, x], load_sem.at[x])
@@ -172,9 +214,9 @@
 
     cell_load = pltpu.make_async_copy(cell_hbm, cell_in, cell_sem)
     cell_load.start()
+    prec_load(prec_x - 1).start()
     main_load(main_x - 1).start()
     main_load(0).start()
-    prec_load(prec_x - 1).start()
     prec_load(0).start()
     for x in range(1, main_x - 1):
         main_load(x).start()
@@ -229,83 +271,62 @@
             src_ref=src, dst_ref=dst, send_sem=send, recv_sem=recv, device_id=device, device_id_type=MESH
         )
 
-    def x_face(g, count, rows, east_side, send, recv):
-        inner = pl.ds(TOP, rows)
-        if east_side:
-            return remote(g.at[2, :, count, :, inner], g.at[2, :, 0, :, inner], send.at[0], recv.at[0], (east, gy))
-        return remote(g.at[0, :, 1, :, inner], g.at[0, :, count + 1, :, inner], send.at[1], recv.at[1], (west, gy))
-
-    main_east = x_face(main_g, main_x, main_y, True, main_send, main_recv)
-    main_west = x_face(main_g, main_x, main_y, False, main_send, main_recv)
-    prec_east = x_face(prec_g, prec_x, prec_y, True, prec_send, prec_recv)
-    prec_west = x_face(prec_g, prec_x, prec_y, False, prec_send, prec_recv)
-
-    def inlet(target):
-        place = pl.ds(pl.multiple_of(TOP + lax.rem(gy, 2) * prec_y, ROWS), prec_y)
-        return remote(
-            prec_g.at[2, :, prec_x, :, pl.ds(TOP, prec_y)],
-            main_g.at[2, :, 0, :, place],
-            extra_send.at[target],
-            main_recv.at[0],
-            (0, lax.div(gy, 2) + target * half),
-        )
-
-    main_load(main_x - 1).wait()
-    cell_load.wait()
-    main_plane(main_x - 1)
-    pl.semaphore_wait(barrier, jnp.where(last, 12, 8))
-
-    @pl.when(jnp.logical_not(last))
-    def _():
-        main_east.start()
-
-    main_load(0).wait()
-    main_plane(0)
-
-    @pl.when(jnp.logical_not(first))
-    def _():
-        main_west.start()
-
-    prec_load(prec_x - 1).wait()
-    prec_plane(prec_x - 1)
-    prec_east.start()
-
-    @pl.when(last)
-    def _():
-        inlet(0).start()
-        inlet(1).start()
-
-    prec_load(0).wait()
-    prec_plane(0)
-    prec_west.start()
-
-    def prec_rest(x, carry):
-        prec_load(x).wait()
-        prec_plane(x)
-        return carry
-
-    lax.fori_loop(1, prec_x - 1, prec_rest, 0)
-
-    def pack(g, count, rows, out_y, out_c):
-        for side in range(2):
-            row = TOP + rows - 1 if side == 0 else TOP
-            for a in range(3):
-                for e in range(3):
-                    i = 9 * a + (6 if side == 0 else 0) + e
-                    for part in range(count * ztiles // ROWS):
-                        out_y[side, 3 * a + e, pl.ds(part * ROWS, ROWS), :] = load_across(g, i, part, row)
-        for corner in range(4):
-            side, a, x = corner % 2, 2 if corner < 2 else 0, count if corner < 2 else 1
-            row = TOP + rows - 1 if side == 0 else TOP
-            for e in range(3):
-                for z in range(ztiles):
-                    out_c[corner, pl.ds(e * ztiles + z, 1), :] = g[a, (6 if side == 0 else 0) + e, x, z, pl.ds(row, 1), :]
-
-    def y_copies(out_y, got_y, send, recv):
-        return [
-            remote(out_y.at[side], got_y.at[side], send.at[2 + side], recv.at[2 + side], (gx, (north, south)[side]))
-            for side in range(2)
-        ]
+    near = ztiles - ztiles // 2
+
+    class Faces:
+        def __init__(self, g, count, rows, send, recv, relay, arrival):
+            inner = pl.ds(TOP, rows)
+            lower, upper = pl.ds(0, near), pl.ds(near, ztiles // 2)
+
+            def face(side, zs):
+                source, dest = (g.at[2, :, count, zs, inner], g.at[2, :, 0, zs, inner])
+                if side:
+                    source, dest = (g.at[0, :, 1, zs, inner], g.at[0, :, count + 1, zs, inner])
+                return source, dest, send.at[side], recv.at[side], (west if side else east, gy)
+
+            whole = pl.ds(0, ztiles)
+            self.whole = [remote(*face(side, whole)) for side in range(2)]
+            self.direct = [remote(*face(side, lower)) for side in range(2)]
+            self.to_relay = [
+                remote(face(side, upper)[0], relay, send.at[8], arrival, (relay_of, gy)) for side in range(2)
+            ]
+            self.from_relay = [
+                remote(relay, face(side, upper)[1], send.at[9], recv.at[side], (relay_to, gy)) for side in range(2)
+            ]
+
+        def start(self, side):
+            split = down_source if side else up_source
+
+            @pl.when(split)
+            def _():
+                self.to_relay[side].start()
+                self.direct[side].start()
+
+            @pl.when(jnp.logical_not(split))
+            def _():
+                self.whole[side].start()
+
+        def wait_send(self, side):
+            split = down_source if side else up_source
+
+            @pl.when(split)
+            def _():
+                self.to_relay[side].wait_send()
+                self.direct[side].wait_send()
+
+            @pl.when(jnp.logical_not(split))
+            def _():
+                self.whole[side].wait_send()
+
+    main_faces = Faces(main_g, main_x, main_y, main_send, main_recv, main_relay, relay_recv.at[0])
+    prec_faces = Faces(prec_g, prec_x, prec_y, prec_send, prec_recv, prec_relay, relay_recv.at[1])
+
+    def pack_corner(g, count, rows, out_c, corner):
+        side, a, x = corner % 2, 2 if corner < 2 else 0, count if corner < 2 else 1
+        row = TOP + rows - 1 if side == 0 else TOP
+        for e in range(3):
+            for z in range(ztiles):
+                out_c[corner, pl.ds(e * ztiles + z, 1), :] = g[a, (6 if side == 0 else 0) + e, x, z, pl.ds(row, 1), :]
 
     def corner_copies(out_c, got_c, send, recv):
         return [
@@ -316,31 +337,79 @@
             for corner in range(4)
         ]
 
-    def inlet_corner(corner, target):
-        block = lax.rem(lax.div(gy + 1, 2), half) if corner == 0 else lax.rem(lax.div(gy, 2) + half - 1, half)
-        return remote(
-            prec_out_c.at[corner], main_got_c.at[corner], extra_send.at[2 + target], main_recv.at[4 + corner],
-            (0, block + target * half),
-        )
-
-    pack(prec_g, prec_x, prec_y, prec_out_y, prec_out_c)
+    prec_corners = corner_copies(prec_out_c, prec_got_c, prec_send, prec_recv)
+    main_corners = corner_copies(main_out_c, main_got_c, main_send, main_recv)
+
+    prec_load(prec_x - 1).wait()
+    prec_plane(prec_x - 1)
+    pack_corner(prec_g, prec_x, prec_y, prec_out_c, 0)
+    pack_corner(prec_g, prec_x, prec_y, prec_out_c, 1)
+    main_load(main_x - 1).wait()
+    cell_load.wait()
+    main_plane(main_x - 1)
+    pack_corner(main_g, main_x, main_y, main_out_c, 0)
+    pack_corner(main_g, main_x, main_y, main_out_c, 1)
+    pl.semaphore_wait(barrier, greetings)
+    prec_corners[0].start()
+    prec_corners[1].start()
+
+    @pl.when(jnp.logical_not(last))
+    def _():
+        main_corners[0].start()
+        main_corners[1].start()
+
+    prec_faces.start(0)
+
+    @pl.when(jnp.logical_not(last))
+    def _():
+        main_faces.start(0)
+
+    main_load(0).wait()
+    main_plane(0)
+    pack_corner(main_g, main_x, main_y, main_out_c, 2)
+    pack_corner(main_g, main_x, main_y, main_out_c, 3)
+
+    @pl.when(jnp.logical_not(first))
+    def _():
+        main_corners[2].start()
+        main_corners[3].start()
+        main_faces.start(1)
+
+    prec_load(0).wait()
+    prec_plane(0)
+    pack_corner(prec_g, prec_x, prec_y, prec_out_c, 2)
+    pack_corner(prec_g, prec_x, prec_y, prec_out_c, 3)
+    prec_corners[2].start()
+    prec_corners[3].start()
+    prec_faces.start(1)
+
+    def prec_rest(x, carry):
+        prec_load(x).wait()
+        prec_plane(x)
+        return carry
+
+    lax.fori_loop(1, prec_x - 1, prec_rest, 0)
+
+    def pack(g, count, rows, out_y):
+        for side in range(2):
+            row = TOP + rows - 1 if side == 0 else TOP
+            for a in range(3):
+                for e in range(3):
+                    i = 9 * a + (6 if side == 0 else 0) + e
+                    for part in range(count * ztiles // ROWS):
+                        out_y[side, 3 * a + e, pl.ds(part * ROWS, ROWS), :] = load_across(g, i, part, row)
+
+    def y_copies(out_y, got_y, send, recv):
+        return [
+            remote(out_y.at[side], got_y.at[side], send.at[2 + side], recv.at[2 + side], (gx, (north, south)[side]))
+            for side in range(2)
+        ]
+
+    pack(prec_g, prec_x, prec_y, prec_out_y)
     prec_y_copies = y_copies(prec_out_y, prec_got_y, prec_send, prec_recv)
-    prec_corners = corner_copies(prec_out_c, prec_got_c, prec_send, prec_recv)
     main_y_copies = y_copies(main_out_y, main_got_y, main_send, main_recv)
-    main_corners = corner_copies(main_out_c, main_got_c, main_send, main_recv)
-    odd = lax.rem(gy, 2) == 1
-    for copy in prec_y_copies + prec_corners:
+    for copy in prec_y_copies:
         copy.start()
-
-    @pl.when(jnp.logical_and(last, odd))
-    def _():
-        inlet_corner(0, 0).start()
-        inlet_corner(0, 1).start()
-
-    @pl.when(jnp.logical_and(last, jnp.logical_not(odd)))
-    def _():
-        inlet_corner(1, 0).start()
-        inlet_corner(1, 1).start()
 
     def main_rest(x, carry):
         main_load(x).wait()
@@ -348,19 +417,64 @@
         return carry
 
     lax.fori_loop(1, main_x - 1, main_rest, 0)
-    pack(main_g, main_x, main_y, main_out_y, main_out_c)
+    pack(main_g, main_x, main_y, main_out_y)
     for copy in main_y_copies:
         copy.start()
 
-    @pl.when(jnp.logical_not(last))
-    def _():
-        main_corners[0].start()
-        main_corners[1].start()
-
-    @pl.when(jnp.logical_not(first))
-    def _():
-        main_corners[2].start()
-        main_corners[3].start()
+    @pl.when(relaying)
+    def _():
+        main_faces.to_relay[0].wait_recv()
+        prec_faces.to_relay[0].wait_recv()
+
+    @pl.when(up_relay)
+    def _():
+        main_faces.from_relay[0].start()
+        prec_faces.from_relay[0].start()
+
+    @pl.when(down_relay)
+    def _():
+        main_faces.from_relay[1].start()
+        prec_faces.from_relay[1].start()
+
+    def inlet_copies(target, run):
+        where = inlet_targets[target]
+        if target < 2:
+            rows = pl.ds(pl.multiple_of(TOP + lax.rem(gy, 2) * prec_y, ROWS), prec_y)
+            pairs = [(True, prec_g.at[2, :, 0, :, pl.ds(TOP, prec_y)], main_g.at[2, :, 0, :, rows], main_recv.at[0])]
+        else:
+            pairs = [
+                (odd if corner == 0 else jnp.logical_not(odd), inlet_c, main_got_c.at[corner], main_recv.at[4 + corner])
+                for corner in range(2)
+            ]
+        for chosen, source, dest, arrival in pairs:
+
+            @pl.when(jnp.logical_and(chosen, where != gy))
+            def _():
+                run(remote(source, dest, inlet_send.at[target], arrival, (0, where)), True)
+
+            @pl.when(jnp.logical_and(chosen, where == gy))
+            def _():
+                run(pltpu.make_async_copy(source, dest, arrival), False)
+
+    @pl.when(first)
+    def _():
+        prec_faces.whole[0].wait_recv()
+        for target in range(2):
+            inlet_copies(target, lambda copy, far: copy.start())
+        for e in range(3):
+            for z in range(ztiles):
+                line = pl.ds(e * ztiles + z, 1)
+
+                @pl.when(odd)
+                def _():
+                    inlet_c[line, :] = prec_g[2, 6 + e, 0, z, pl.ds(TOP + prec_y - 1, 1), :]
+
+                @pl.when(jnp.logical_not(odd))
+                def _():
+                    inlet_c[line, :] = prec_g[2, e, 0, z, pl.ds(TOP, 1), :]
+
+        for target in range(2, 4):
+            inlet_copies(target, lambda copy, far: copy.start())
 
     def unpack(g, count, rows, got_y):
         for side in range(2):
@@ -397,32 +511,51 @@
             main_corners[corner].wait_recv()
             unpack_corner(main_g, main_x, main_y, main_got_c, corner)
 
-    prec_east.wait_recv()
-    prec_west.wait_recv()
-    main_east.wait_recv()
+    @pl.when(jnp.logical_not(first))
+    def _():
+        prec_faces.whole[0].wait_recv()
+
+    prec_faces.whole[1].wait_recv()
+    main_faces.whole[0].wait_recv()
 
     @pl.when(jnp.logical_not(last))
     def _():
-        main_west.wait_recv()
-
-    for copy in [prec_east, prec_west, *prec_y_copies, *prec_corners, *main_y_copies]:
+        main_faces.whole[1].wait_recv()
+
+    for copy in [*prec_y_copies, *prec_corners, *main_y_copies]:
         copy.wait_send()
+    prec_faces.wait_send(0)
+    prec_faces.wait_send(1)
 
     @pl.when(jnp.logical_not(last))
     def _():
-        for copy in (main_east, main_corners[0], main_corners[1]):
-            copy.wait_send()
+        main_corners[0].wait_send()
+        main_corners[1].wait_send()
+        main_faces.wait_send(0)
 
     @pl.when(jnp.logical_not(first))
     def _():
-        for copy in (main_west, main_corners[2], main_corners[3]):
-            copy.wait_send()
-
-    @pl.when(last)
-    def _():
-        for target in range(2):
-            inlet(target).wait_send()
-            inlet_corner(0, target).wait_send()
+        main_corners[2].wait_send()
+        main_corners[3].wait_send()
+        main_faces.wait_send(1)
+
+    @pl.when(relaying)
+    def _():
+        main_faces.from_relay[0].wait_send()
+        prec_faces.from_relay[0].wait_send()
+
+    @pl.when(first)
+    def _():
+        for target in range(4):
+
+            @pl.when(inlet_targets[target] != gy)
+            def _():
+                if target < 2:
+                    inlet_copies(target, lambda copy, far: copy.wait_send() if far else None)
+                else:
+                    remote(
+                        inlet_c, main_got_c.at[0], inlet_send.at[target], main_recv.at[4], (0, inlet_targets[target])
+                    ).wait_send()
 
 
 def stream(nx, main_g, prec_g, prec_next, main_next, prec_out, main_out, prec_sem, main_sem):
@@ -513,11 +646,15 @@
                 pltpu.VMEM((4, ROWS, LANES), F32),
                 pltpu.SemaphoreType.DMA((main_x + prec_x,)),
                 pltpu.SemaphoreType.DMA,
+                pltpu.SemaphoreType.DMA((10,)),
                 pltpu.SemaphoreType.DMA((8,)),
-                pltpu.SemaphoreType.DMA((8,)),
-                pltpu.SemaphoreType.DMA((8,)),
+                pltpu.SemaphoreType.DMA((10,)),
                 pltpu.SemaphoreType.DMA((8,)),
                 pltpu.SemaphoreType.DMA((4,)),
+                pltpu.VMEM((ROWS, LANES), F32),
+                pltpu.VMEM((9, ztiles // 2, main_y, LANES), F32),
+                pltpu.VMEM((9, ztiles // 2, prec_y, LANES), F32),
+                pltpu.SemaphoreType.DMA((2,)),
             ],
             compiler_params=pltpu.CompilerParams(
                 collective_id=0, has_side_effects=True, vmem_limit_bytes=24 * 1024 * 1024

time: 30.5 us -> 26.6 us (0.87)
  the two profiles are of different devices: /device:TPU:33 before, /device:TPU:2 now
where the time goes in v1:
time: 26.6 us; the launch traced here: 26.5 us
  Pallas kernels  25.9 us (97%)
  between operations  0.64 us (2%)
    pallas_call x1, Pallas kernels, shards(): pl.pallas_call(functools.partial(exchange, (nx, ny)), name='exchange', ou...  22.9 us
    pallas_call x1, Pallas kernels, shards(): pl.pallas_call(functools.partial(stream, nx), name='stream', out_shape=(j...  3.02 us

profile of v1, /device:TPU:2, one launch (start us, length us, event | category | flops | bytes accessed | tf_op | source)
XLA Modules:
  0.0 26.5 jit_solution(2665236276779325611)
XLA Ops:
  0.6 22.9 %exchange.1 = (f32[3,9,10,2,32,128]{5,4,3,2,1,0:T(8,128)S(1)}, f32[3,9,6,2,24,128]{5,4,3,2,1,0:T(8,128)S(1)}) custom-call(f32[27]{0:T(128)} %rates.1, f32[27,4,8,256]{3,2,1,0:T(8,128)} %prec_hbm.1, f32[27,8,16,256]{3,2,1,0:T(8,128)} %main_hbm.1, s32[8,16,256]{2,1,0:T(8,128)} %cell_hbm.1), custom_call_target="tpu_custom_call" | custom-call | tf_op jit(solution)/shard_map/exchange/pallas_call | solution.py:628
  23.5 3.0 %stream.1 = (f32[27,4,8,256]{3,2,1,0:T(8,128)}, f32[27,8,16,256]{3,2,1,0:T(8,128)}) custom-call(f32[3,9,10,2,32,128]{5,4,3,2,1,0:T(8,128)S(1)} %get-tuple-element.4.main_g, f32[3,9,6,2,24,128]{5,4,3,2,1,0:T(8,128)S(1)} %get-tuple-element.5.prec_g), custom_call_target="tpu_custom_call" | custom-call | tf_op jit(solution)/shard_map/stream/pallas_call | solution.py:663

commit v2 on v1

--- a/solution.py
+++ b/solution.py
@@ -127,23 +127,27 @@
     table,
     main_out_y,
     main_got_y,
-    main_out_c,
-    main_got_c,
     prec_out_y,
     prec_got_y,
-    prec_out_c,
-    prec_got_c,
+    packet,
+    packet_x,
+    packet_y,
+    inlet_c,
+    main_relay,
+    prec_relay,
+    inlet_relay,
     load_sem,
     cell_sem,
     main_send,
     main_recv,
     prec_send,
     prec_recv,
+    packet_send,
+    packet_recv,
     inlet_send,
-    inlet_c,
-    main_relay,
-    prec_relay,
+    inlet_recv,
     relay_recv,
+    late_ready,
 ):
     nx, ny = size
     gx, gy = lax.axis_index("gx"), lax.axis_index("gy")
@@ -151,13 +155,14 @@
     prec_x, prec_y = prec_in.shape[1], prec_in.shape[2]
     ztiles = main_g.shape[3]
     first, last = gx == 0, gx == nx - 1
+    inner_first, inner_last = jnp.logical_not(first), jnp.logical_not(last)
     east, west = lax.rem(gx + 1, nx), lax.rem(gx + nx - 1, nx)
     north, south = lax.rem(gy + 1, ny), lax.rem(gy + ny - 1, ny)
     half = ny // 2
 
     place = lax.rem(gx, GROUP)
-    up_source = jnp.logical_and(place == GROUP - 1, jnp.logical_not(last))
-    down_source = jnp.logical_and(place == 0, jnp.logical_not(first))
+    up_source = jnp.logical_and(place == GROUP - 1, inner_last)
+    down_source = jnp.logical_and(place == 0, inner_first)
     up_relay = jnp.logical_and(place == 0, gx + GROUP < nx)
     down_relay = jnp.logical_and(place == GROUP - 1, gx - GROUP >= 0)
     crossing = jnp.logical_or(up_source, down_source)
@@ -167,21 +172,23 @@
     relay_of = jnp.where(up_source, gx - GROUP + 1, gx + GROUP - 1)
     relay_back = jnp.where(down_source, gx - GROUP, gx + GROUP)
 
+    passing = gx == nx - GROUP
     odd = lax.rem(gy, 2) == 1
+    inlet_block = lax.div(gy, 2)
     corner_block = jnp.where(odd, lax.rem(lax.div(gy + 1, 2), half), lax.rem(lax.div(gy, 2) + half - 1, half))
-    inlet_targets = [lax.div(gy, 2), lax.div(gy, 2) + half, corner_block, corner_block + half]
 
     barrier = pltpu.get_barrier_semaphore()
 
     def greet(device):
         pl.semaphore_signal(barrier, inc=1, device_id=device, device_id_type=MESH)
 
-    for other in (
-        (west, gy), (east, gy), (gx, south), (gx, north),
-        (west, south), (west, north), (east, south), (east, north),
-    ):
+    for other in ((west, gy), (gx, south), (gx, north)):
         greet(other)
 
+    @pl.when(inner_last)
+    def _():
+        greet((east, gy))
+
     @pl.when(relaying)
     def _():
         greet((relay_from, gy))
@@ -190,21 +197,22 @@
     def _():
         greet((relay_back, gy))
 
+    @pl.when(passing)
+    def _():
+        greet((nx - 1, gy))
+
     @pl.when(first)
     def _():
-        for block in (2 * gy, 2 * gy + 1, 2 * gy + ny - 1, 2 * gy + 2):
-            source = lax.rem(block, ny)
-
-            @pl.when(source != gy)
-            def _():
-                greet((0, source))
+        source = jnp.where(gy < half, nx - 1, nx - GROUP)
+        greet((source, lax.rem(2 * gy, ny)))
+        greet((source, lax.rem(2 * gy + 1, ny)))
+        greet((nx - 1, lax.rem(2 * gy + ny - 1, ny)))
+        greet((nx - 1, lax.rem(2 * gy + 2, ny)))
 
     def one_if(condition):
         return jnp.where(condition, 1, 0)
 
-    greetings = 8 + one_if(relaying) + one_if(crossing)
-    for target in inlet_targets:
-        greetings = greetings + one_if(jnp.logical_and(first, target != gy))
+    greetings = 3 + one_if(inner_first) + one_if(relaying) + one_if(crossing) + one_if(passing) + 4 * one_if(last)
 
     def main_load(x):
         return pltpu.make_async_copy(main_hbm.at[:, x], main_in.at[:, x], load_sem.at[x])
@@ -213,8 +221,8 @@
         return pltpu.make_async_copy(prec_hbm.at[:, x], prec_in.at[:, x], load_sem.at[main_x + x])
 
     cell_load = pltpu.make_async_copy(cell_hbm, cell_in, cell_sem)
+    prec_load(prec_x - 1).start()
     cell_load.start()
-    prec_load(prec_x - 1).start()
     main_load(main_x - 1).start()
     main_load(0).start()
     prec_load(0).start()
@@ -288,100 +296,123 @@
             self.whole = [remote(*face(side, whole)) for side in range(2)]
             self.direct = [remote(*face(side, lower)) for side in range(2)]
             self.to_relay = [
-                remote(face(side, upper)[0], relay, send.at[8], arrival, (relay_of, gy)) for side in range(2)
+                remote(face(side, upper)[0], relay, send.at[4], arrival, (relay_of, gy)) for side in range(2)
             ]
             self.from_relay = [
-                remote(relay, face(side, upper)[1], send.at[9], recv.at[side], (relay_to, gy)) for side in range(2)
+                remote(relay, face(side, upper)[1], send.at[5], recv.at[side], (relay_to, gy)) for side in range(2)
             ]
 
-        def start(self, side):
+        def run(self, side, act):
             split = down_source if side else up_source
 
             @pl.when(split)
             def _():
-                self.to_relay[side].start()
-                self.direct[side].start()
+                act(self.to_relay[side])
+                act(self.direct[side])
 
             @pl.when(jnp.logical_not(split))
             def _():
-                self.whole[side].start()
-
-        def wait_send(self, side):
-            split = down_source if side else up_source
-
-            @pl.when(split)
-            def _():
-                self.to_relay[side].wait_send()
-                self.direct[side].wait_send()
-
-            @pl.when(jnp.logical_not(split))
-            def _():
-                self.whole[side].wait_send()
+                act(self.whole[side])
+
+    def start(copy):
+        copy.start()
+
+    def sent(copy):
+        copy.wait_send()
 
     main_faces = Faces(main_g, main_x, main_y, main_send, main_recv, main_relay, relay_recv.at[0])
     prec_faces = Faces(prec_g, prec_x, prec_y, prec_send, prec_recv, prec_relay, relay_recv.at[1])
 
-    def pack_corner(g, count, rows, out_c, corner):
-        side, a, x = corner % 2, 2 if corner < 2 else 0, count if corner < 2 else 1
-        row = TOP + rows - 1 if side == 0 else TOP
-        for e in range(3):
-            for z in range(ztiles):
-                out_c[corner, pl.ds(e * ztiles + z, 1), :] = g[a, (6 if side == 0 else 0) + e, x, z, pl.ds(row, 1), :]
-
-    def corner_copies(out_c, got_c, send, recv):
-        return [
+    def pack_corners(lattice, side):
+        g, count, rows = ((main_g, main_x, main_y), (prec_g, prec_x, prec_y))[lattice]
+        a, x = (0, 1) if side else (2, count)
+        for up in range(2):
+            row = TOP if up else TOP + rows - 1
+            for e in range(3):
+                for z in range(ztiles):
+                    line = g[a, (0 if up else 6) + e, x, z, pl.ds(row, 1), :]
+                    packet[side, up, lattice, pl.ds(e * ztiles + z, 1), :] = line
+
+    packets_x = [
+        remote(packet.at[side], packet_x.at[side], packet_send.at[side], packet_recv.at[side], ((east, west)[side], gy))
+        for side in range(2)
+    ]
+    packets_y = [
+        remote(
+            packet_x.at[:, up], packet_y.at[up], packet_send.at[2 + up], packet_recv.at[2 + up], (gx, (north, south)[up])
+        )
+        for up in range(2)
+    ]
+
+    inlet_rows = pl.ds(pl.multiple_of(TOP + lax.rem(gy, 2) * prec_y, ROWS), prec_y)
+    outlet = prec_g.at[2, :, prec_x, :, pl.ds(TOP, prec_y)]
+    inlet_direct = remote(
+        outlet, main_g.at[2, :, 0, :, inlet_rows], inlet_send.at[0], main_recv.at[0], (0, inlet_block)
+    )
+    inlet_to_relay = remote(outlet, inlet_relay, inlet_send.at[1], relay_recv.at[2], (nx - GROUP, gy))
+    inlet_from_relay = remote(
+        inlet_relay, main_g.at[2, :, 0, :, inlet_rows], inlet_send.at[0], main_recv.at[0], (0, inlet_block + half)
+    )
+    inlet_corners = [
+        [
             remote(
-                out_c.at[corner], got_c.at[corner], send.at[4 + corner], recv.at[4 + corner],
-                (east if corner < 2 else west, (north, south)[corner % 2]),
+                packet.at[0, up, 1], inlet_c.at[up], inlet_send.at[2 + target], inlet_recv.at[up],
+                (0, corner_block + target * half),
             )
-            for corner in range(4)
+            for target in range(2)
         ]
-
-    prec_corners = corner_copies(prec_out_c, prec_got_c, prec_send, prec_recv)
-    main_corners = corner_copies(main_out_c, main_got_c, main_send, main_recv)
+        for up in range(2)
+    ]
+
+    def inlet_run(act):
+        act(inlet_to_relay)
+        act(inlet_direct)
+        for up, chosen in ((0, odd), (1, jnp.logical_not(odd))):
+
+            @pl.when(chosen)
+            def _():
+                act(inlet_corners[up][0])
+                act(inlet_corners[up][1])
 
     prec_load(prec_x - 1).wait()
     prec_plane(prec_x - 1)
-    pack_corner(prec_g, prec_x, prec_y, prec_out_c, 0)
-    pack_corner(prec_g, prec_x, prec_y, prec_out_c, 1)
+    pack_corners(1, 0)
+
+    @pl.when(last)
+    def _():
+        pl.semaphore_wait(barrier, greetings)
+        pl.semaphore_signal(late_ready, inc=1, device_id=(0, gy), device_id_type=MESH)
+        inlet_run(start)
+        prec_faces.whole[0].start()
+
     main_load(main_x - 1).wait()
     cell_load.wait()
     main_plane(main_x - 1)
-    pack_corner(main_g, main_x, main_y, main_out_c, 0)
-    pack_corner(main_g, main_x, main_y, main_out_c, 1)
-    pl.semaphore_wait(barrier, greetings)
-    prec_corners[0].start()
-    prec_corners[1].start()
-
-    @pl.when(jnp.logical_not(last))
-    def _():
-        main_corners[0].start()
-        main_corners[1].start()
-
-    prec_faces.start(0)
-
-    @pl.when(jnp.logical_not(last))
-    def _():
-        main_faces.start(0)
+    pack_corners(0, 0)
+
+    @pl.when(inner_last)
+    def _():
+        pl.semaphore_wait(barrier, greetings)
+
+    packets_x[0].start()
+
+    @pl.when(inner_last)
+    def _():
+        main_faces.run(0, start)
+        prec_faces.run(0, start)
 
     main_load(0).wait()
     main_plane(0)
-    pack_corner(main_g, main_x, main_y, main_out_c, 2)
-    pack_corner(main_g, main_x, main_y, main_out_c, 3)
-
-    @pl.when(jnp.logical_not(first))
-    def _():
-        main_corners[2].start()
-        main_corners[3].start()
-        main_faces.start(1)
-
+    pack_corners(0, 1)
     prec_load(0).wait()
     prec_plane(0)
-    pack_corner(prec_g, prec_x, prec_y, prec_out_c, 2)
-    pack_corner(prec_g, prec_x, prec_y, prec_out_c, 3)
-    prec_corners[2].start()
-    prec_corners[3].start()
-    prec_faces.start(1)
+    pack_corners(1, 1)
+
+    @pl.when(inner_first)
+    def _():
+        packets_x[1].start()
+        main_faces.run(1, start)
+        prec_faces.run(1, start)
 
     def prec_rest(x, carry):
         prec_load(x).wait()
@@ -424,57 +455,42 @@
     @pl.when(relaying)
     def _():
         main_faces.to_relay[0].wait_recv()
+
+    @pl.when(up_relay)
+    def _():
+        main_faces.from_relay[0].start()
+
+    @pl.when(down_relay)
+    def _():
+        main_faces.from_relay[1].start()
+
+    @pl.when(relaying)
+    def _():
         prec_faces.to_relay[0].wait_recv()
 
     @pl.when(up_relay)
     def _():
-        main_faces.from_relay[0].start()
         prec_faces.from_relay[0].start()
 
     @pl.when(down_relay)
     def _():
-        main_faces.from_relay[1].start()
         prec_faces.from_relay[1].start()
 
-    def inlet_copies(target, run):
-        where = inlet_targets[target]
-        if target < 2:
-            rows = pl.ds(pl.multiple_of(TOP + lax.rem(gy, 2) * prec_y, ROWS), prec_y)
-            pairs = [(True, prec_g.at[2, :, 0, :, pl.ds(TOP, prec_y)], main_g.at[2, :, 0, :, rows], main_recv.at[0])]
-        else:
-            pairs = [
-                (odd if corner == 0 else jnp.logical_not(odd), inlet_c, main_got_c.at[corner], main_recv.at[4 + corner])
-                for corner in range(2)
-            ]
-        for chosen, source, dest, arrival in pairs:
-
-            @pl.when(jnp.logical_and(chosen, where != gy))
-            def _():
-                run(remote(source, dest, inlet_send.at[target], arrival, (0, where)), True)
-
-            @pl.when(jnp.logical_and(chosen, where == gy))
-            def _():
-                run(pltpu.make_async_copy(source, dest, arrival), False)
+    @pl.when(passing)
+    def _():
+        inlet_to_relay.wait_recv()
+        inlet_from_relay.start()
 
     @pl.when(first)
     def _():
-        prec_faces.whole[0].wait_recv()
-        for target in range(2):
-            inlet_copies(target, lambda copy, far: copy.start())
-        for e in range(3):
-            for z in range(ztiles):
-                line = pl.ds(e * ztiles + z, 1)
-
-                @pl.when(odd)
-                def _():
-                    inlet_c[line, :] = prec_g[2, 6 + e, 0, z, pl.ds(TOP + prec_y - 1, 1), :]
-
-                @pl.when(jnp.logical_not(odd))
-                def _():
-                    inlet_c[line, :] = prec_g[2, e, 0, z, pl.ds(TOP, 1), :]
-
-        for target in range(2, 4):
-            inlet_copies(target, lambda copy, far: copy.start())
+        pl.semaphore_wait(late_ready, 1)
+        packets_x[1].start()
+        prec_faces.whole[1].start()
+
+    for side in range(2):
+        packets_x[side].wait_recv()
+    for up in range(2):
+        packets_y[up].start()
 
     def unpack(g, count, rows, got_y):
         for side in range(2):
@@ -485,77 +501,68 @@
                     for part in range(count * ztiles // ROWS):
                         store_across(g, i, part, row, got_y[side, 3 * a + e, pl.ds(part * ROWS, ROWS), :])
 
-    def unpack_corner(g, count, rows, got_c, corner):
-        side, a, x = corner % 2, 2 if corner < 2 else 0, 0 if corner < 2 else count + 1
-        row = TOP - 1 if side == 0 else TOP + rows
+    def unpack_corner(lattice, side, up, tile):
+        g, count, rows = ((main_g, main_x, main_y), (prec_g, prec_x, prec_y))[lattice]
+        a, x = (0, count + 1) if side else (2, 0)
+        row = TOP + rows if up else TOP - 1
         for e in range(3):
             for z in range(ztiles):
-                g[a, (6 if side == 0 else 0) + e, x, z, pl.ds(row, 1), :] = got_c[corner, pl.ds(e * ztiles + z, 1), :]
+                g[a, (0 if up else 6) + e, x, z, pl.ds(row, 1), :] = tile[pl.ds(e * ztiles + z, 1), :]
 
     for side in range(2):
         prec_y_copies[side].wait_recv()
     unpack(prec_g, prec_x, prec_y, prec_got_y)
-    for corner in range(4):
-        prec_corners[corner].wait_recv()
-        unpack_corner(prec_g, prec_x, prec_y, prec_got_c, corner)
     for side in range(2):
         main_y_copies[side].wait_recv()
     unpack(main_g, main_x, main_y, main_got_y)
-    for corner in range(2):
-        main_corners[corner].wait_recv()
-        unpack_corner(main_g, main_x, main_y, main_got_c, corner)
-
-    @pl.when(jnp.logical_not(last))
-    def _():
-        for corner in range(2, 4):
-            main_corners[corner].wait_recv()
-            unpack_corner(main_g, main_x, main_y, main_got_c, corner)
-
-    @pl.when(jnp.logical_not(first))
-    def _():
-        prec_faces.whole[0].wait_recv()
-
+    for up in range(2):
+        packets_y[up].wait_recv()
+        for side in range(2):
+            unpack_corner(1, side, up, packet_y.at[up, side, 1])
+        unpack_corner(0, 1, up, packet_y.at[up, 1, 0])
+
+        @pl.when(inner_first)
+        def _():
+            unpack_corner(0, 0, up, packet_y.at[up, 0, 0])
+
+        @pl.when(first)
+        def _():
+            inlet_corners[up][0].wait_recv()
+            unpack_corner(0, 0, up, inlet_c.at[up])
+
+    prec_faces.whole[0].wait_recv()
     prec_faces.whole[1].wait_recv()
     main_faces.whole[0].wait_recv()
 
-    @pl.when(jnp.logical_not(last))
+    @pl.when(inner_last)
     def _():
         main_faces.whole[1].wait_recv()
 
-    for copy in [*prec_y_copies, *prec_corners, *main_y_copies]:
+    for copy in [*prec_y_copies, *main_y_copies, *packets_x, *packets_y]:
         copy.wait_send()
-    prec_faces.wait_send(0)
-    prec_faces.wait_send(1)
-
-    @pl.when(jnp.logical_not(last))
-    def _():
-        main_corners[0].wait_send()
-        main_corners[1].wait_send()
-        main_faces.wait_send(0)
-
-    @pl.when(jnp.logical_not(first))
-    def _():
-        main_corners[2].wait_send()
-        main_corners[3].wait_send()
-        main_faces.wait_send(1)
+    prec_faces.run(0, sent)
+    prec_faces.run(1, sent)
+
+    @pl.when(inner_last)
+    def _():
+        main_faces.run(0, sent)
+
+    @pl.when(inner_first)
+    def _():
+        main_faces.run(1, sent)
 
     @pl.when(relaying)
     def _():
         main_faces.from_relay[0].wait_send()
         prec_faces.from_relay[0].wait_send()
 
-    @pl.when(first)
-    def _():
-        for target in range(4):
-
-            @pl.when(inlet_targets[target] != gy)
-            def _():
-                if target < 2:
-                    inlet_copies(target, lambda copy, far: copy.wait_send() if far else None)
-                else:
-                    remote(
-                        inlet_c, main_got_c.at[0], inlet_send.at[target], main_recv.at[4], (0, inlet_targets[target])
-                    ).wait_send()
+    @pl.when(passing)
+    def _():
+        inlet_from_relay.wait_send()
+
+    @pl.when(last)
+    def _():
+        inlet_run(sent)
 
 
 def stream(nx, main_g, prec_g, prec_next, main_next, prec_out, main_out, prec_sem, main_sem):
@@ -638,23 +645,27 @@
                 pltpu.VMEM((54, ROWS, LANES), F32),
                 pltpu.VMEM((2, 9, main_x * ztiles, LANES), F32),
                 pltpu.VMEM((2, 9, main_x * ztiles, LANES), F32),
-                pltpu.VMEM((4, ROWS, LANES), F32),
-                pltpu.VMEM((4, ROWS, LANES), F32),
                 pltpu.VMEM((2, 9, prec_x * ztiles, LANES), F32),
                 pltpu.VMEM((2, 9, prec_x * ztiles, LANES), F32),
-                pltpu.VMEM((4, ROWS, LANES), F32),
-                pltpu.VMEM((4, ROWS, LANES), F32),
+                pltpu.VMEM((2, 2, 2, ROWS, LANES), F32),
+                pltpu.VMEM((2, 2, 2, ROWS, LANES), F32),
+                pltpu.VMEM((2, 2, 2, ROWS, LANES), F32),
+                pltpu.VMEM((2, ROWS, LANES), F32),
+                pltpu.VMEM((9, ztiles // 2, main_y, LANES), F32),
+                pltpu.VMEM((9, ztiles // 2, prec_y, LANES), F32),
+                pltpu.VMEM((9, ztiles, prec_y, LANES), F32),
                 pltpu.SemaphoreType.DMA((main_x + prec_x,)),
                 pltpu.SemaphoreType.DMA,
-                pltpu.SemaphoreType.DMA((10,)),
-                pltpu.SemaphoreType.DMA((8,)),
-                pltpu.SemaphoreType.DMA((10,)),
-                pltpu.SemaphoreType.DMA((8,)),
+                pltpu.SemaphoreType.DMA((6,)),
                 pltpu.SemaphoreType.DMA((4,)),
-                pltpu.VMEM((ROWS, LANES), F32),
-                pltpu.VMEM((9, ztiles // 2, main_y, LANES), F32),
-                pltpu.VMEM((9, ztiles // 2, prec_y, LANES), F32),
+                pltpu.SemaphoreType.DMA((6,)),
+                pltpu.SemaphoreType.DMA((4,)),
+                pltpu.SemaphoreType.DMA((4,)),
+                pltpu.SemaphoreType.DMA((4,)),
+                pltpu.SemaphoreType.DMA((4,)),
                 pltpu.SemaphoreType.DMA((2,)),
+                pltpu.SemaphoreType.DMA((3,)),
+                pltpu.SemaphoreType.REGULAR,
             ],
             compiler_params=pltpu.CompilerParams(
                 collective_id=0, has_side_effects=True, vmem_limit_bytes=24 * 1024 * 1024

time: 26.6 us -> 26.9 us (1.011)
  the two profiles are of different devices: /device:TPU:2 before, /device:TPU:1 now
where the time goes in v2:
time: 26.9 us; the launch traced here: 26.8 us
  Pallas kernels  26.2 us (97%)
  between operations  0.64 us (2%)
    pallas_call x1, Pallas kernels, shards(): pl.pallas_call(functools.partial(exchange, (nx, ny)), name='exchange', ou...  23.2 us
    pallas_call x1, Pallas kernels, shards(): pl.pallas_call(functools.partial(stream, nx), name='stream', out_shape=(j...  3.02 us

profile of v2, /device:TPU:1, one launch (start us, length us, event | category | flops | bytes accessed | tf_op | source)
XLA Modules:
  0.0 26.8 jit_solution(1769602254037341845)
XLA Ops:
  0.6 23.2 %exchange.1 = (f32[3,9,10,2,32,128]{5,4,3,2,1,0:T(8,128)S(1)}, f32[3,9,6,2,24,128]{5,4,3,2,1,0:T(8,128)S(1)}) custom-call(f32[27]{0:T(128)} %rates.1, f32[27,4,8,256]{3,2,1,0:T(8,128)} %prec_hbm.1, f32[27,8,16,256]{3,2,1,0:T(8,128)} %main_hbm.1, s32[8,16,256]{2,1,0:T(8,128)} %cell_hbm.1), custom_call_target="tpu_custom_call" | custom-call | tf_op jit(solution)/shard_map/exchange/pallas_call | solution.py:635
  23.8 3.0 %stream.1 = (f32[27,4,8,256]{3,2,1,0:T(8,128)}, f32[27,8,16,256]{3,2,1,0:T(8,128)}) custom-call(f32[3,9,10,2,32,128]{5,4,3,2,1,0:T(8,128)S(1)} %get-tuple-element.4.main_g, f32[3,9,6,2,24,128]{5,4,3,2,1,0:T(8,128)S(1)} %get-tuple-element.5.prec_g), custom_call_target="tpu_custom_call" | custom-call | tf_op jit(solution)/shard_map/stream/pallas_call | solution.py:674

commit v3 on v2

--- a/solution.py
+++ b/solution.py
@@ -113,6 +113,37 @@
     flat[rows, :] = value
 
 
+def stream_plane(g, out, slot, count, x, clamp):
+    lane = lax.broadcasted_iota(jnp.int32, (ROWS, LANES), 1)
+    low, high = lane == 0, lane == LANES - 1
+    ztiles = g.shape[3]
+
+    def body(step, carry):
+        row = pl.multiple_of(step * ROWS, ROWS)
+        for i in range(27):
+            cx, cy, cz = i // 9 - 1, i // 3 % 3 - 1, i % 3 - 1
+            source = x + 1 - cx
+            if clamp is not None and cx == -1:
+                source = jnp.where(clamp, jnp.minimum(source, count), source)
+            tiles = [g[i // 9, i % 9, source, z, pl.ds(TOP - cy + row, ROWS), :] for z in range(ztiles)]
+            if cz:
+                j = 26 - i
+                wall = 0 if cz == 1 else ztiles - 1
+                bounced = g[j // 9, j % 9, x + 1, wall, pl.ds(pl.multiple_of(TOP + row, ROWS), ROWS), :]
+                moved = [pltpu.roll(tile, 1 if cz == 1 else LANES - 1, 1) for tile in tiles]
+                if cz == 1:
+                    tiles = [jnp.where(low, moved[z - 1] if z else bounced, moved[z]) for z in range(ztiles)]
+                else:
+                    tiles = [
+                        jnp.where(high, moved[z + 1] if z < ztiles - 1 else bounced, moved[z]) for z in range(ztiles)
+                    ]
+            for z in range(ztiles):
+                out[slot, i, pl.ds(row, ROWS), pl.ds(z * LANES, LANES)] = tiles[z]
+        return carry
+
+    lax.fori_loop(0, out.shape[2] // ROWS, body, 0)
+
+
 def exchange(
     size,
     rates,
@@ -121,6 +152,8 @@
     cell_hbm,
     main_g,
     prec_g,
+    main_mid,
+    prec_mid,
     main_in,
     prec_in,
     cell_in,
@@ -148,6 +181,7 @@
     inlet_recv,
     relay_recv,
     late_ready,
+    near_ready,
 ):
     nx, ny = size
     gx, gy = lax.axis_index("gx"), lax.axis_index("gy")
@@ -177,23 +211,35 @@
     inlet_block = lax.div(gy, 2)
     corner_block = jnp.where(odd, lax.rem(lax.div(gy + 1, 2), half), lax.rem(lax.div(gy, 2) + half - 1, half))
 
+    beside_last = gx == nx - 2
+    below_last = gx == nx - 1 - GROUP
     barrier = pltpu.get_barrier_semaphore()
 
     def greet(device):
         pl.semaphore_signal(barrier, inc=1, device_id=device, device_id_type=MESH)
 
-    for other in ((west, gy), (gx, south), (gx, north)):
-        greet(other)
+    greet((west, gy))
+
+    @pl.when(last)
+    def _():
+        greet((west, south))
+        greet((west, north))
+        greet((gx - GROUP, gy))
 
     @pl.when(inner_last)
     def _():
+        greet((gx, south))
+        greet((gx, north))
+
+    @pl.when(gx < nx - 2)
+    def _():
         greet((east, gy))
 
     @pl.when(relaying)
     def _():
         greet((relay_from, gy))
 
-    @pl.when(crossing)
+    @pl.when(jnp.logical_and(crossing, jnp.logical_not(below_last)))
     def _():
         greet((relay_back, gy))
 
@@ -208,11 +254,14 @@
         greet((source, lax.rem(2 * gy + 1, ny)))
         greet((nx - 1, lax.rem(2 * gy + ny - 1, ny)))
         greet((nx - 1, lax.rem(2 * gy + 2, ny)))
+        greet((nx - 1, south))
+        greet((nx - 1, north))
 
     def one_if(condition):
         return jnp.where(condition, 1, 0)
 
-    greetings = 3 + one_if(inner_first) + one_if(relaying) + one_if(crossing) + one_if(passing) + 4 * one_if(last)
+    greetings = 3 + one_if(inner_first) + one_if(relaying) + one_if(crossing) + one_if(passing)
+    greetings = jnp.where(last, 7, greetings + 2 * one_if(beside_last) + one_if(below_last))
 
     def main_load(x):
         return pltpu.make_async_copy(main_hbm.at[:, x], main_in.at[:, x], load_sem.at[x])
@@ -230,6 +279,11 @@
         main_load(x).start()
     for x in range(1, prec_x - 1):
         prec_load(x).start()
+
+    @pl.when(last)
+    def _():
+        pl.semaphore_wait(barrier, greetings)
+        pl.semaphore_signal(late_ready, inc=1, device_id=(0, gy), device_id_type=MESH)
 
     for k in range(27):
         rate = rates[k]
@@ -340,6 +394,21 @@
     packets_y = [
         remote(
             packet_x.at[:, up], packet_y.at[up], packet_send.at[2 + up], packet_recv.at[2 + up], (gx, (north, south)[up])
+        )
+        for up in range(2)
+    ]
+
+    wrap_corners = [
+        remote(
+            packet.at[0, up, 1], packet_y.at[up, 0, 1], inlet_send.at[4 + up], inlet_recv.at[2 + up],
+            (0, (north, south)[up]),
+        )
+        for up in range(2)
+    ]
+    west_packets_y = [
+        remote(
+            packet_x.at[1, up], packet_y.at[up, 1], packet_send.at[2 + up], packet_recv.at[2 + up],
+            (gx, (north, south)[up]),
         )
         for up in range(2)
     ]
@@ -365,6 +434,8 @@
     ]
 
     def inlet_run(act):
+        act(wrap_corners[0])
+        act(wrap_corners[1])
         act(inlet_to_relay)
         act(inlet_direct)
         for up, chosen in ((0, odd), (1, jnp.logical_not(odd))):
@@ -380,8 +451,6 @@
 
     @pl.when(last)
     def _():
-        pl.semaphore_wait(barrier, greetings)
-        pl.semaphore_signal(late_ready, inc=1, device_id=(0, gy), device_id_type=MESH)
         inlet_run(start)
         prec_faces.whole[0].start()
 
@@ -394,10 +463,21 @@
     def _():
         pl.semaphore_wait(barrier, greetings)
 
-    packets_x[0].start()
+    def ready(device):
+        pl.semaphore_signal(near_ready, inc=1, device_id=device, device_id_type=MESH)
+
+    @pl.when(beside_last)
+    def _():
+        for row in (gy, south, north):
+            ready((nx - 1, row))
+
+    @pl.when(below_last)
+    def _():
+        ready((nx - 1, gy))
 
     @pl.when(inner_last)
     def _():
+        packets_x[0].start()
         main_faces.run(0, start)
         prec_faces.run(0, start)
 
@@ -407,6 +487,10 @@
     prec_load(0).wait()
     prec_plane(0)
     pack_corners(1, 1)
+
+    @pl.when(last)
+    def _():
+        pl.semaphore_wait(near_ready, 4)
 
     @pl.when(inner_first)
     def _():
@@ -481,16 +565,18 @@
         inlet_to_relay.wait_recv()
         inlet_from_relay.start()
 
+    packets_x[1].wait_recv()
+
+    @pl.when(inner_first)
+    def _():
+        packets_x[0].wait_recv()
+        for up in range(2):
+            packets_y[up].start()
+
     @pl.when(first)
     def _():
-        pl.semaphore_wait(late_ready, 1)
-        packets_x[1].start()
-        prec_faces.whole[1].start()
-
-    for side in range(2):
-        packets_x[side].wait_recv()
-    for up in range(2):
-        packets_y[up].start()
+        for up in range(2):
+            west_packets_y[up].start()
 
     def unpack(g, count, rows, got_y):
         for side in range(2):
@@ -515,20 +601,41 @@
     for side in range(2):
         main_y_copies[side].wait_recv()
     unpack(main_g, main_x, main_y, main_got_y)
+
+    def main_middle(x, carry):
+        stream_plane(main_g, main_mid, x - 1, main_x, x, None)
+        return carry
+
+    def prec_middle(x, carry):
+        stream_plane(prec_g, prec_mid, x - 1, prec_x, x, None)
+        return carry
+
+    lax.fori_loop(1, main_x - 1, main_middle, 0)
+    lax.fori_loop(1, prec_x - 1, prec_middle, 0)
+
+    @pl.when(first)
+    def _():
+        pl.semaphore_wait(late_ready, 1)
+        packets_x[1].start()
+        prec_faces.whole[1].start()
+
     for up in range(2):
-        packets_y[up].wait_recv()
+
+        @pl.when(inner_first)
+        def _():
+            packets_y[up].wait_recv()
+            unpack_corner(0, 0, up, packet_y.at[up, 0, 0])
+
+        @pl.when(first)
+        def _():
+            west_packets_y[up].wait_recv()
+            wrap_corners[up].wait_recv()
+            inlet_corners[up][0].wait_recv()
+            unpack_corner(0, 0, up, inlet_c.at[up])
+
+        unpack_corner(0, 1, up, packet_y.at[up, 1, 0])
         for side in range(2):
             unpack_corner(1, side, up, packet_y.at[up, side, 1])
-        unpack_corner(0, 1, up, packet_y.at[up, 1, 0])
-
-        @pl.when(inner_first)
-        def _():
-            unpack_corner(0, 0, up, packet_y.at[up, 0, 0])
-
-        @pl.when(first)
-        def _():
-            inlet_corners[up][0].wait_recv()
-            unpack_corner(0, 0, up, inlet_c.at[up])
 
     prec_faces.whole[0].wait_recv()
     prec_faces.whole[1].wait_recv()
@@ -538,18 +645,26 @@
     def _():
         main_faces.whole[1].wait_recv()
 
-    for copy in [*prec_y_copies, *main_y_copies, *packets_x, *packets_y]:
+    for copy in [*prec_y_copies, *main_y_copies, packets_x[1]]:
         copy.wait_send()
     prec_faces.run(0, sent)
     prec_faces.run(1, sent)
 
     @pl.when(inner_last)
     def _():
+        packets_x[0].wait_send()
         main_faces.run(0, sent)
 
     @pl.when(inner_first)
     def _():
+        for up in range(2):
+            packets_y[up].wait_send()
         main_faces.run(1, sent)
+
+    @pl.when(first)
+    def _():
+        for up in range(2):
+            west_packets_y[up].wait_send()
 
     @pl.when(relaying)
     def _():
@@ -565,60 +680,24 @@
         inlet_run(sent)
 
 
-def stream(nx, main_g, prec_g, prec_next, main_next, prec_out, main_out, prec_sem, main_sem):
+def stream(nx, main_g, prec_g, main_mid, prec_mid, prec_next, main_next, prec_out, main_out, prec_sem, main_sem):
     last = lax.axis_index("gx") == nx - 1
-
-    def plane(g, out, count, rows, x, clamp):
-        lane = lax.broadcasted_iota(jnp.int32, (ROWS, LANES), 1)
-        low, high = lane == 0, lane == LANES - 1
-        ztiles = g.shape[3]
-
-        def body(step, carry):
-            row = pl.multiple_of(step * ROWS, ROWS)
-            for i in range(27):
-                cx, cy, cz = i // 9 - 1, i // 3 % 3 - 1, i % 3 - 1
-                source = x + 1 - cx
-                if clamp and cx == -1:
-                    source = jnp.where(last, jnp.minimum(source, count), source)
-                tiles = [g[i // 9, i % 9, source, z, pl.ds(TOP - cy + row, ROWS), :] for z in range(ztiles)]
-                if cz:
-                    j = 26 - i
-                    wall = 0 if cz == 1 else ztiles - 1
-                    bounced = g[j // 9, j % 9, x + 1, wall, pl.ds(pl.multiple_of(TOP + row, ROWS), ROWS), :]
-                    moved = [pltpu.roll(tile, 1 if cz == 1 else LANES - 1, 1) for tile in tiles]
-                    if cz == 1:
-                        tiles = [jnp.where(low, moved[z - 1] if z else bounced, moved[z]) for z in range(ztiles)]
-                    else:
-                        tiles = [
-                            jnp.where(high, moved[z + 1] if z < ztiles - 1 else bounced, moved[z])
-                            for z in range(ztiles)
-                        ]
-                for z in range(ztiles):
-                    out[x, i, pl.ds(row, ROWS), pl.ds(z * LANES, LANES)] = tiles[z]
-            return carry
-
-        lax.fori_loop(0, rows // ROWS, body, 0)
-
-    def run(g, out, dest, sem, clamp):
-        count, rows = out.shape[0], out.shape[2]
-
-        def copy(x):
-            return pltpu.make_async_copy(out.at[x], dest.at[:, x], sem.at[x])
-
-        def body(x, carry):
-            plane(g, out, count, rows, x, clamp)
-            copy(x).start()
-            return carry
-
-        lax.fori_loop(0, count, body, 0)
-        return copy
-
-    main_copy = run(main_g, main_out, main_next, main_sem, True)
-    prec_copy = run(prec_g, prec_out, prec_next, prec_sem, False)
-    for x in range(main_out.shape[0]):
-        main_copy(x).wait()
-    for x in range(prec_out.shape[0]):
-        prec_copy(x).wait()
+    copies = []
+    for mid, dest, sem in ((main_mid, main_next, main_sem), (prec_mid, prec_next, prec_sem)):
+        for x in range(1, dest.shape[1] - 1):
+            copies.append(pltpu.make_async_copy(mid.at[x - 1], dest.at[:, x], sem.at[x]))
+            copies[-1].start()
+    for g, out, dest, sem, clamp in (
+        (main_g, main_out, main_next, main_sem, last),
+        (prec_g, prec_out, prec_next, prec_sem, None),
+    ):
+        count = dest.shape[1]
+        for slot, x in enumerate((0, count - 1)):
+            stream_plane(g, out, slot, count, x, clamp)
+            copies.append(pltpu.make_async_copy(out.at[slot], dest.at[:, x], sem.at[x]))
+            copies[-1].start()
+    for copy in copies:
+        copy.wait()
 
 
 def solution(mesh):
@@ -632,12 +711,17 @@
         prec_shape = (3, 9, prec_x + 2, ztiles, prec_y + 2 * TOP, LANES)
         in_hbm = pl.BlockSpec(memory_space=pltpu.HBM)
         on_chip = pl.BlockSpec(memory_space=pltpu.VMEM)
-        main_g, prec_g = pl.pallas_call(
+        main_g, prec_g, main_mid, prec_mid = pl.pallas_call(
             functools.partial(exchange, (nx, ny)),
             name="exchange",
-            out_shape=(pltpu.VMEM(main_shape, F32), pltpu.VMEM(prec_shape, F32)),
+            out_shape=(
+                pltpu.VMEM(main_shape, F32),
+                pltpu.VMEM(prec_shape, F32),
+                pltpu.VMEM((main_x - 2, 27, main_y, depth), F32),
+                pltpu.VMEM((prec_x - 2, 27, prec_y, depth), F32),
+            ),
             in_specs=[pl.BlockSpec(memory_space=pltpu.SMEM), in_hbm, in_hbm, in_hbm],
-            out_specs=(on_chip, on_chip),
+            out_specs=(on_chip,) * 4,
             scratch_shapes=[
                 pltpu.VMEM(main_pops.shape, F32),
                 pltpu.VMEM(prec_pops.shape, F32),
@@ -662,9 +746,10 @@
                 pltpu.SemaphoreType.DMA((4,)),
                 pltpu.SemaphoreType.DMA((4,)),
                 pltpu.SemaphoreType.DMA((4,)),
+                pltpu.SemaphoreType.DMA((6,)),
                 pltpu.SemaphoreType.DMA((4,)),
-                pltpu.SemaphoreType.DMA((2,)),
                 pltpu.SemaphoreType.DMA((3,)),
+                pltpu.SemaphoreType.REGULAR,
                 pltpu.SemaphoreType.REGULAR,
             ],
             compiler_params=pltpu.CompilerParams(
@@ -678,16 +763,16 @@
                 jax.ShapeDtypeStruct(prec_pops.shape, F32),
                 jax.ShapeDtypeStruct(main_pops.shape, F32),
             ),
-            in_specs=[on_chip, on_chip],
+            in_specs=[on_chip] * 4,
             out_specs=(in_hbm, in_hbm),
             scratch_shapes=[
-                pltpu.VMEM((prec_x, 27, prec_y, depth), F32),
-                pltpu.VMEM((main_x, 27, main_y, depth), F32),
+                pltpu.VMEM((2, 27, prec_y, depth), F32),
+                pltpu.VMEM((2, 27, main_y, depth), F32),
                 pltpu.SemaphoreType.DMA((prec_x,)),
                 pltpu.SemaphoreType.DMA((main_x,)),
             ],
             compiler_params=pltpu.CompilerParams(vmem_limit_bytes=24 * 1024 * 1024),
-        )(main_g, prec_g)
+        )(main_g, prec_g, main_mid, prec_mid)
         return prec_next, main_next
 
     placed = (P(None, "gx", "gy", None), P(None, "gx", "gy", None), P("gx", "gy", None), P())

time: 26.9 us -> 22 us (0.82)
  the two profiles are of different devices: /device:TPU:1 before, /device:TPU:2 now
where the time goes in v3:
time: 22 us; the launch traced here: 21.9 us
  Pallas kernels  21.2 us (96%)
  between operations  0.64 us (3%)
    pallas_call x1, Pallas kernels, shards(): pl.pallas_call(functools.partial(exchange, (nx, ny)), name='exchange', ou...  19.1 us
    pallas_call x1, Pallas kernels, shards(): pl.pallas_call(functools.partial(stream, nx), name='stream', out_shape=(j...  2.18 us

profile of v3, /device:TPU:2, one launch (start us, length us, event | category | flops | bytes accessed | tf_op | source)
XLA Modules:
  0.0 21.9 jit_solution(9794566905898621820)
XLA Ops:
  0.6 19.1 %exchange.1 = (f32[3,9,10,2,32,128]{5,4,3,2,1,0:T(8,128)S(1)}, f32[3,9,6,2,24,128]{5,4,3,2,1,0:T(8,128)S(1)}, f32[6,27,16,256]{3,2,1,0:T(8,128)S(1)}, f32[2,27,8,256]{3,2,1,0:T(8,128)S(1)}) custom-call(f32[27]{0:T(128)} %rates.1, f32[27,4,8,256]{3,2,1,0:T(8,128)} %prec_hbm.1, f32[27,8,16,256]{3,2,1,0:T(8,128)} %main_hbm.1, s32[8,16,256]{2,1,0:T(8,128)} %cell_hbm.1), custom_call_target="tpu_custom_call" | custom-call | tf_op jit(solution)/shard_map/exchange/pallas_call | solution.py:714
  19.7 2.2 %stream.1 = (f32[27,4,8,256]{3,2,1,0:T(8,128)}, f32[27,8,16,256]{3,2,1,0:T(8,128)}) custom-call(f32[3,9,10,2,32,128]{5,4,3,2,1,0:T(8,128)S(1)} %get-tuple-element.6.main_g, f32[3,9,6,2,24,128]{5,4,3,2,1,0:T(8,128)S(1)} %get-tuple-element.7.prec_g, f32[6,27,16,256]{3,2,1,0:T(8,128)S(1)} %get-tuple-element.8.main_mid, ...), custom_call_target="tpu_custom_call" | custom-call | tf_op jit(solution)/shard_map/stream/pallas_call | solution.py:759

commit v4 on v3

--- a/solution.py
+++ b/solution.py
@@ -200,6 +200,10 @@
     up_relay = jnp.logical_and(place == 0, gx + GROUP < nx)
     down_relay = jnp.logical_and(place == GROUP - 1, gx - GROUP >= 0)
     crossing = jnp.logical_or(up_source, down_source)
+    up_second = place == GROUP - 2
+    down_second = jnp.logical_and(place == 1, gx >= 2)
+    second = jnp.logical_or(up_second, down_second)
+    second_to = jnp.where(up_second, lax.rem(gx + 2, nx), gx - 2)
     relaying = jnp.logical_or(up_relay, down_relay)
     relay_from = jnp.where(up_relay, gx + GROUP - 1, gx - GROUP + 1)
     relay_to = jnp.where(up_relay, gx + GROUP, gx - GROUP)
@@ -211,6 +215,10 @@
     inlet_block = lax.div(gy, 2)
     corner_block = jnp.where(odd, lax.rem(lax.div(gy + 1, 2), half), lax.rem(lax.div(gy, 2) + half - 1, half))
 
+    straight = jnp.logical_and(last, lax.rem(gy, 4) == 0)
+    passing_face = jnp.logical_and(gx == nx - 2, lax.rem(gy, 4) != 0)
+
+    holding = gx == GROUP - 1
     beside_last = gx == nx - 2
     below_last = gx == nx - 1 - GROUP
     barrier = pltpu.get_barrier_semaphore()
@@ -231,10 +239,16 @@
         greet((gx, south))
         greet((gx, north))
 
-    @pl.when(gx < nx - 2)
-    def _():
         greet((east, gy))
 
+    @pl.when(place == 0)
+    def _():
+        greet((lax.rem(gx + nx - 2, nx), gy))
+
+    @pl.when(up_source)
+    def _():
+        greet((gx + 2, gy))
+
     @pl.when(relaying)
     def _():
         greet((relay_from, gy))
@@ -243,9 +257,13 @@
     def _():
         greet((relay_back, gy))
 
-    @pl.when(passing)
+    @pl.when(jnp.logical_or(passing, holding))
     def _():
         greet((nx - 1, gy))
+
+    @pl.when(holding)
+    def _():
+        greet((0, gy))
 
     @pl.when(first)
     def _():
@@ -260,8 +278,9 @@
     def one_if(condition):
         return jnp.where(condition, 1, 0)
 
-    greetings = 3 + one_if(inner_first) + one_if(relaying) + one_if(crossing) + one_if(passing)
-    greetings = jnp.where(last, 7, greetings + 2 * one_if(beside_last) + one_if(below_last))
+    greetings = 3 + one_if(inner_first) + one_if(relaying) + one_if(crossing) + one_if(passing) + one_if(second)
+    greetings = greetings + one_if(first)
+    greetings = jnp.where(last, 9, greetings + 2 * one_if(beside_last) + one_if(below_last))
 
     def main_load(x):
         return pltpu.make_async_copy(main_hbm.at[:, x], main_in.at[:, x], load_sem.at[x])
@@ -284,6 +303,7 @@
     def _():
         pl.semaphore_wait(barrier, greetings)
         pl.semaphore_signal(late_ready, inc=1, device_id=(0, gy), device_id_type=MESH)
+        pl.semaphore_signal(late_ready, inc=1, device_id=(GROUP - 1, gy), device_id_type=MESH)
 
     for k in range(27):
         rate = rates[k]
@@ -335,26 +355,24 @@
 
     near = ztiles - ztiles // 2
 
-    class Faces:
-        def __init__(self, g, count, rows, send, recv, relay, arrival):
-            inner = pl.ds(TOP, rows)
-            lower, upper = pl.ds(0, near), pl.ds(near, ztiles // 2)
-
-            def face(side, zs):
-                source, dest = (g.at[2, :, count, zs, inner], g.at[2, :, 0, zs, inner])
-                if side:
-                    source, dest = (g.at[0, :, 1, zs, inner], g.at[0, :, count + 1, zs, inner])
-                return source, dest, send.at[side], recv.at[side], (west if side else east, gy)
-
-            whole = pl.ds(0, ztiles)
-            self.whole = [remote(*face(side, whole)) for side in range(2)]
-            self.direct = [remote(*face(side, lower)) for side in range(2)]
+    def face(g, count, rows, side, zs, send, recv):
+        inner = pl.ds(TOP, rows)
+        source, dest = (g.at[2, :, count, zs, inner], g.at[2, :, 0, zs, inner])
+        if side:
+            source, dest = (g.at[0, :, 1, zs, inner], g.at[0, :, count + 1, zs, inner])
+        return source, dest, send.at[side], recv.at[side], (west if side else east, gy)
+
+    class MainFaces:
+        def __init__(self):
+            whole, lower, upper = pl.ds(0, ztiles), pl.ds(0, near), pl.ds(near, ztiles // 2)
+            parts = (main_g, main_x, main_y)
+            self.whole = [remote(*face(*parts, side, whole, main_send, main_recv)) for side in range(2)]
+            self.direct = [remote(*face(*parts, side, lower, main_send, main_recv)) for side in range(2)]
+            ends = [face(*parts, side, upper, main_send, main_recv) for side in range(2)]
             self.to_relay = [
-                remote(face(side, upper)[0], relay, send.at[4], arrival, (relay_of, gy)) for side in range(2)
+                remote(end[0], main_relay, main_send.at[4], relay_recv.at[0], (relay_of, gy)) for end in ends
             ]
-            self.from_relay = [
-                remote(relay, face(side, upper)[1], send.at[5], recv.at[side], (relay_to, gy)) for side in range(2)
-            ]
+            self.from_relay = [remote(main_relay, end[1], main_send.at[5], end[3], (relay_to, gy)) for end in ends]
 
         def run(self, side, act):
             split = down_source if side else up_source
@@ -368,14 +386,37 @@
             def _():
                 act(self.whole[side])
 
+    class PrecFaces:
+        def __init__(self):
+            ends = [face(prec_g, prec_x, prec_y, side, pl.ds(0, ztiles), prec_send, prec_recv) for side in range(2)]
+            self.whole = [remote(*end) for end in ends]
+            self.to_relay = [
+                remote(ends[side][0], prec_relay, prec_send.at[4], relay_recv.at[1], ((west, east)[side], gy))
+                for side in range(2)
+            ]
+            self.from_relay = [remote(prec_relay, end[1], prec_send.at[5], end[3], (second_to, gy)) for end in ends]
+            self.west_to_hold = remote(
+                ends[1][0], prec_relay, prec_send.at[1], relay_recv.at[1], (GROUP - 1, gy)
+            )
+            self.west_from_hold = remote(prec_relay, ends[1][1], prec_send.at[5], ends[1][3], (nx - 1, gy))
+        def run(self, side, act):
+            split = down_source if side else up_source
+
+            @pl.when(split)
+            def _():
+                act(self.to_relay[side])
+
+            @pl.when(jnp.logical_not(split))
+            def _():
+                act(self.whole[side])
+
     def start(copy):
         copy.start()
 
     def sent(copy):
         copy.wait_send()
 
-    main_faces = Faces(main_g, main_x, main_y, main_send, main_recv, main_relay, relay_recv.at[0])
-    prec_faces = Faces(prec_g, prec_x, prec_y, prec_send, prec_recv, prec_relay, relay_recv.at[1])
+    main_faces, prec_faces = MainFaces(), PrecFaces()
 
     def pack_corners(lattice, side):
         g, count, rows = ((main_g, main_x, main_y), (prec_g, prec_x, prec_y))[lattice]
@@ -436,8 +477,6 @@
     def inlet_run(act):
         act(wrap_corners[0])
         act(wrap_corners[1])
-        act(inlet_to_relay)
-        act(inlet_direct)
         for up, chosen in ((0, odd), (1, jnp.logical_not(odd))):
 
             @pl.when(chosen)
@@ -445,6 +484,18 @@
                 act(inlet_corners[up][0])
                 act(inlet_corners[up][1])
 
+        act(inlet_to_relay)
+
+        @pl.when(jnp.logical_not(straight))
+        def _():
+            act(prec_faces.to_relay[0])
+
+        act(inlet_direct)
+
+        @pl.when(straight)
+        def _():
+            act(prec_faces.whole[0])
+
     prec_load(prec_x - 1).wait()
     prec_plane(prec_x - 1)
     pack_corners(1, 0)
@@ -452,7 +503,6 @@
     @pl.when(last)
     def _():
         inlet_run(start)
-        prec_faces.whole[0].start()
 
     main_load(main_x - 1).wait()
     cell_load.wait()
@@ -478,6 +528,9 @@
     @pl.when(inner_last)
     def _():
         packets_x[0].start()
+
+    @pl.when(jnp.logical_and(inner_last, jnp.logical_not(down_source)))
+    def _():
         main_faces.run(0, start)
         prec_faces.run(0, start)
 
@@ -495,8 +548,17 @@
     @pl.when(inner_first)
     def _():
         packets_x[1].start()
+        prec_faces.run(1, start)
         main_faces.run(1, start)
-        prec_faces.run(1, start)
+
+    @pl.when(first)
+    def _():
+        prec_faces.west_to_hold.start()
+
+    @pl.when(down_source)
+    def _():
+        main_faces.run(0, start)
+        prec_faces.run(0, start)
 
     def prec_rest(x, carry):
         prec_load(x).wait()
@@ -531,7 +593,19 @@
         main_plane(x)
         return carry
 
-    lax.fori_loop(1, main_x - 1, main_rest, 0)
+    lax.fori_loop(1, main_x // 2, main_rest, 0)
+
+    @pl.when(passing)
+    def _():
+        inlet_to_relay.wait_recv()
+        inlet_from_relay.start()
+
+    @pl.when(passing_face)
+    def _():
+        prec_faces.to_relay[0].wait_recv()
+        prec_faces.from_relay[0].start()
+
+    lax.fori_loop(main_x // 2, main_x - 1, main_rest, 0)
     pack(main_g, main_x, main_y, main_out_y)
     for copy in main_y_copies:
         copy.start()
@@ -548,22 +622,17 @@
     def _():
         main_faces.from_relay[1].start()
 
-    @pl.when(relaying)
+    @pl.when(jnp.logical_and(second, jnp.logical_not(beside_last)))
     def _():
         prec_faces.to_relay[0].wait_recv()
 
-    @pl.when(up_relay)
+    @pl.when(jnp.logical_and(up_second, jnp.logical_not(beside_last)))
     def _():
         prec_faces.from_relay[0].start()
 
-    @pl.when(down_relay)
+    @pl.when(down_second)
     def _():
         prec_faces.from_relay[1].start()
-
-    @pl.when(passing)
-    def _():
-        inlet_to_relay.wait_recv()
-        inlet_from_relay.start()
 
     packets_x[1].wait_recv()
 
@@ -617,7 +686,12 @@
     def _():
         pl.semaphore_wait(late_ready, 1)
         packets_x[1].start()
-        prec_faces.whole[1].start()
+
+    @pl.when(holding)
+    def _():
+        prec_faces.west_to_hold.wait_recv()
+        pl.semaphore_wait(late_ready, 1)
+        prec_faces.west_from_hold.start()
 
     for up in range(2):
 
@@ -647,11 +721,18 @@
 
     for copy in [*prec_y_copies, *main_y_copies, packets_x[1]]:
         copy.wait_send()
-    prec_faces.run(0, sent)
-    prec_faces.run(1, sent)
+
+    @pl.when(first)
+    def _():
+        prec_faces.west_to_hold.wait_send()
+
+    @pl.when(holding)
+    def _():
+        prec_faces.west_from_hold.wait_send()
 
     @pl.when(inner_last)
     def _():
+        prec_faces.run(0, sent)
         packets_x[0].wait_send()
         main_faces.run(0, sent)
 
@@ -660,6 +741,7 @@
         for up in range(2):
             packets_y[up].wait_send()
         main_faces.run(1, sent)
+        prec_faces.run(1, sent)
 
     @pl.when(first)
     def _():
@@ -669,6 +751,9 @@
     @pl.when(relaying)
     def _():
         main_faces.from_relay[0].wait_send()
+
+    @pl.when(jnp.logical_or(passing_face, jnp.logical_and(second, jnp.logical_not(beside_last))))
+    def _():
         prec_faces.from_relay[0].wait_send()
 
     @pl.when(passing)
@@ -736,7 +821,7 @@
                 pltpu.VMEM((2, 2, 2, ROWS, LANES), F32),
                 pltpu.VMEM((2, ROWS, LANES), F32),
                 pltpu.VMEM((9, ztiles // 2, main_y, LANES), F32),
-                pltpu.VMEM((9, ztiles // 2, prec_y, LANES), F32),
+                pltpu.VMEM((9, ztiles, prec_y, LANES), F32),
                 pltpu.VMEM((9, ztiles, prec_y, LANES), F32),
                 pltpu.SemaphoreType.DMA((main_x + prec_x,)),
                 pltpu.SemaphoreType.DMA,

time: 22 us -> 20.9 us (0.950)
  Pallas kernels: 21.2 us -> 19.9 us
    pallas_call x1, Pallas kernels: 19.1 us -> 17.7 us  [shards(): pl.pallas_call(functools.partial(exchange, (nx, ny)), name='exchange', ou...]
where the time goes in v4:
time: 20.9 us; the launch traced here: 20.6 us
  Pallas kernels  19.9 us (95%)
  between operations  0.64 us (3%)
    pallas_call x1, Pallas kernels, shards(): pl.pallas_call(functools.partial(exchange, (nx, ny)), name='exchange', ou...  17.7 us
    pallas_call x1, Pallas kernels, shards(): pl.pallas_call(functools.partial(stream, nx), name='stream', out_shape=(j...  2.18 us

profile of v4, /device:TPU:2, one launch (start us, length us, event | category | flops | bytes accessed | tf_op | source)
XLA Modules:
  0.0 20.6 jit_solution(5009997081182860649)
XLA Ops:
  0.6 17.7 %exchange.1 = (f32[3,9,10,2,32,128]{5,4,3,2,1,0:T(8,128)S(1)}, f32[3,9,6,2,24,128]{5,4,3,2,1,0:T(8,128)S(1)}, f32[6,27,16,256]{3,2,1,0:T(8,128)S(1)}, f32[2,27,8,256]{3,2,1,0:T(8,128)S(1)}) custom-call(f32[27]{0:T(128)} %rates.1, f32[27,4,8,256]{3,2,1,0:T(8,128)} %prec_hbm.1, f32[27,8,16,256]{3,2,1,0:T(8,128)} %main_hbm.1, s32[8,16,256]{2,1,0:T(8,128)} %cell_hbm.1), custom_call_target="tpu_custom_call" | custom-call | tf_op jit(solution)/shard_map/exchange/pallas_call | solution.py:799
  18.4 2.2 %stream.1 = (f32[27,4,8,256]{3,2,1,0:T(8,128)}, f32[27,8,16,256]{3,2,1,0:T(8,128)}) custom-call(f32[3,9,10,2,32,128]{5,4,3,2,1,0:T(8,128)S(1)} %get-tuple-element.6.main_g, f32[3,9,6,2,24,128]{5,4,3,2,1,0:T(8,128)S(1)} %get-tuple-element.7.prec_g, f32[6,27,16,256]{3,2,1,0:T(8,128)S(1)} %get-tuple-element.8.main_mid, ...), custom_call_target="tpu_custom_call" | custom-call | tf_op jit(solution)/shard_map/stream/pallas_call | solution.py:844

commit v5 on v4

--- a/solution.py
+++ b/solution.py
@@ -146,7 +146,7 @@
 
 def exchange(
     size,
-    rates,
+    rates_hbm,
     prec_hbm,
     main_hbm,
     cell_hbm,
@@ -182,6 +182,8 @@
     relay_recv,
     late_ready,
     near_ready,
+    rates,
+    rates_sem,
 ):
     nx, ny = size
     gx, gy = lax.axis_index("gx"), lax.axis_index("gy")
@@ -289,6 +291,8 @@
         return pltpu.make_async_copy(prec_hbm.at[:, x], prec_in.at[:, x], load_sem.at[main_x + x])
 
     cell_load = pltpu.make_async_copy(cell_hbm, cell_in, cell_sem)
+    rates_load = pltpu.make_async_copy(rates_hbm, rates, rates_sem)
+    rates_load.start()
     prec_load(prec_x - 1).start()
     cell_load.start()
     main_load(main_x - 1).start()
@@ -305,6 +309,7 @@
         pl.semaphore_signal(late_ready, inc=1, device_id=(0, gy), device_id_type=MESH)
         pl.semaphore_signal(late_ready, inc=1, device_id=(GROUP - 1, gy), device_id_type=MESH)
 
+    rates_load.wait()
     for k in range(27):
         rate = rates[k]
         kept = scale_of(k) * (1.0 - rate)
@@ -805,7 +810,7 @@
                 pltpu.VMEM((main_x - 2, 27, main_y, depth), F32),
                 pltpu.VMEM((prec_x - 2, 27, prec_y, depth), F32),
             ),
-            in_specs=[pl.BlockSpec(memory_space=pltpu.SMEM), in_hbm, in_hbm, in_hbm],
+            in_specs=[in_hbm] * 4,
             out_specs=(on_chip,) * 4,
             scratch_shapes=[
                 pltpu.VMEM(main_pops.shape, F32),
@@ -836,6 +841,8 @@
                 pltpu.SemaphoreType.DMA((3,)),
                 pltpu.SemaphoreType.REGULAR,
                 pltpu.SemaphoreType.REGULAR,
+                pltpu.SMEM((27,), F32),
+                pltpu.SemaphoreType.DMA,
             ],
             compiler_params=pltpu.CompilerParams(
                 collective_id=0, has_side_effects=True, vmem_limit_bytes=24 * 1024 * 1024

time: 20.9 us -> 20.2 us (0.967)
  Pallas kernels: 19.9 us -> 19.3 us
    pallas_call x1, Pallas kernels: 17.7 us -> 17.1 us  [shards(): pl.pallas_call(functools.partial(exchange, (nx, ny)), name='exchange', ou...]
where the time goes in v5:
time: 20.2 us; the launch traced here: 19.9 us
  Pallas kernels  19.3 us (96%)
  between operations  0.64 us (3%)
    pallas_call x1, Pallas kernels, shards(): pl.pallas_call(functools.partial(exchange, (nx, ny)), name='exchange', ou...  17.1 us
    pallas_call x1, Pallas kernels, shards(): pl.pallas_call(functools.partial(stream, nx), name='stream', out_shape=(j...  2.18 us

profile of v5, /device:TPU:2, one launch (start us, length us, event | category | flops | bytes accessed | tf_op | source)
XLA Modules:
  0.0 19.9 jit_solution(11282601481642887120)
XLA Ops:
  0.6 17.1 %exchange.1 = (f32[3,9,10,2,32,128]{5,4,3,2,1,0:T(8,128)S(1)}, f32[3,9,6,2,24,128]{5,4,3,2,1,0:T(8,128)S(1)}, f32[6,27,16,256]{3,2,1,0:T(8,128)S(1)}, f32[2,27,8,256]{3,2,1,0:T(8,128)S(1)}) custom-call(f32[27]{0:T(128)} %rates_hbm.1, f32[27,4,8,256]{3,2,1,0:T(8,128)} %prec_hbm.1, f32[27,8,16,256]{3,2,1,0:T(8,128)} %main_hbm.1, s32[8,16,256]{2,1,0:T(8,128)} %cell_hbm.1), custom_call_target="tpu_custom_call" | custom-call | tf_op jit(solution)/shard_map/exchange/pallas_call | solution.py:804
  17.7 2.2 %stream.1 = (f32[27,4,8,256]{3,2,1,0:T(8,128)}, f32[27,8,16,256]{3,2,1,0:T(8,128)}) custom-call(f32[3,9,10,2,32,128]{5,4,3,2,1,0:T(8,128)S(1)} %get-tuple-element.6.main_g, f32[3,9,6,2,24,128]{5,4,3,2,1,0:T(8,128)S(1)} %get-tuple-element.7.prec_g, f32[6,27,16,256]{3,2,1,0:T(8,128)S(1)} %get-tuple-element.8.main_mid, ...), custom_call_target="tpu_custom_call" | custom-call | tf_op jit(solution)/shard_map/stream/pallas_call | solution.py:851

commit v6 on v5

--- a/solution.py
+++ b/solution.py
@@ -217,8 +217,9 @@
     inlet_block = lax.div(gy, 2)
     corner_block = jnp.where(odd, lax.rem(lax.div(gy + 1, 2), half), lax.rem(lax.div(gy, 2) + half - 1, half))
 
-    straight = jnp.logical_and(last, lax.rem(gy, 4) == 0)
-    passing_face = jnp.logical_and(gx == nx - 2, lax.rem(gy, 4) != 0)
+    straight_row = jnp.logical_and(lax.rem(gy, 4) == 0, gy > 0)
+    straight = jnp.logical_and(last, straight_row)
+    passing_face = jnp.logical_and(gx == nx - 2, jnp.logical_not(straight_row))
 
     holding = gx == GROUP - 1
     beside_last = gx == nx - 2
@@ -489,13 +490,12 @@
                 act(inlet_corners[up][0])
                 act(inlet_corners[up][1])
 
+        act(inlet_direct)
         act(inlet_to_relay)
 
         @pl.when(jnp.logical_not(straight))
         def _():
             act(prec_faces.to_relay[0])
-
-        act(inlet_direct)
 
         @pl.when(straight)
         def _():

time: 20.2 us -> 20.2 us (level)
  no operation moved by 1% of the time
where the time goes in v6:
time: 20.2 us; the launch traced here: 19.9 us
  Pallas kernels  19.3 us (96%)
  between operations  0.64 us (3%)
    pallas_call x1, Pallas kernels, shards(): pl.pallas_call(functools.partial(exchange, (nx, ny)), name='exchange', ou...  17.1 us
    pallas_call x1, Pallas kernels, shards(): pl.pallas_call(functools.partial(stream, nx), name='stream', out_shape=(j...  2.18 us

profile of v6, /device:TPU:2, one launch (start us, length us, event | category | flops | bytes accessed | tf_op | source)
XLA Modules:
  0.0 19.9 jit_solution(2097228460163070147)
XLA Ops:
  0.6 17.1 %exchange.1 = (f32[3,9,10,2,32,128]{5,4,3,2,1,0:T(8,128)S(1)}, f32[3,9,6,2,24,128]{5,4,3,2,1,0:T(8,128)S(1)}, f32[6,27,16,256]{3,2,1,0:T(8,128)S(1)}, f32[2,27,8,256]{3,2,1,0:T(8,128)S(1)}) custom-call(f32[27]{0:T(128)} %rates_hbm.1, f32[27,4,8,256]{3,2,1,0:T(8,128)} %prec_hbm.1, f32[27,8,16,256]{3,2,1,0:T(8,128)} %main_hbm.1, s32[8,16,256]{2,1,0:T(8,128)} %cell_hbm.1), custom_call_target="tpu_custom_call" | custom-call | tf_op jit(solution)/shard_map/exchange/pallas_call | solution.py:804
  17.7 2.2 %stream.1 = (f32[27,4,8,256]{3,2,1,0:T(8,128)}, f32[27,8,16,256]{3,2,1,0:T(8,128)}) custom-call(f32[3,9,10,2,32,128]{5,4,3,2,1,0:T(8,128)S(1)} %get-tuple-element.6.main_g, f32[3,9,6,2,24,128]{5,4,3,2,1,0:T(8,128)S(1)} %get-tuple-element.7.prec_g, f32[6,27,16,256]{3,2,1,0:T(8,128)S(1)} %get-tuple-element.8.main_mid, ...), custom_call_target="tpu_custom_call" | custom-call | tf_op jit(solution)/shard_map/stream/pallas_call | solution.py:851
